TPU v7x, 128 devices: a whole 4x4x4 slice. The times are simulated.
128 devices in a mesh: base: 16 (over z, y), freq: 8 (over x, core).
Axes of the slice: x: 4, y: 4, z: 4, core: 2. Of those that a mesh axis runs over, the one named last changes fastest.
Arguments:
- visibilities: bfloat16 [2, 16384, 2048], P(None, 'base', 'freq'), may hold values from -0.01171875 to 0.01171875
- anchor: bfloat16 [2, 16384], P(None, 'base'), may hold values from 4 to 60, as said below
- drift: bfloat16 [2, 16384], P(None, 'base'), may hold values from -0.01953125 to 0.01953125
- target: int32 [16384, 1], P('base'), may hold values from 0 to 127; in each aligned block of 1024 rows (0 to 1023, 1024 to 2047, ...) at most 8 rows name the same one
- subgrid_w: float32 [128], P('base'), may hold values from -1 to 1
- facet_owner: int32 [128, 1], P('base'), may hold values from 0 to 15; in each aligned block of 8 rows (0 to 7, 8 to 15, ...) at most 2 rows name the same one
- row_offset: int32 [128], P('base'), may hold values from 0 to 64
- col_offset: int32 [128], P('base'), may hold values from 0 to 16320
Outputs:
- grid: float32 [2, 2048, 16384], P(None, 'base')
Inputs may be any that keep to these rules, and one draw needn't show every extreme that they name: `target`: among the 1024 blocks of one index of base no subgrid is named more than 8 times. `facet_owner`: among the 8 subgrids of one index of base no owner is named more than 2 times. anchor[k,b] + 2048 drift[k,b] lies between 4 and 60, up to the rounding of drift.
All inputs are finite; a program needn't handle non-finite values.
Results may differ from a plain program's by a relative error of at most 0.0038.
Values may be sent and summed in bfloat16 or wider, within the bound.
A program may use at most 128 MiB of HBM per device.

v0:
```python
import math

import jax
import jax.numpy as jnp
from jax import lax
from jax.sharding import PartitionSpec as P

G = 64
GY = 16384
CAP = 8
FCAP = 2
FR = 128


def slot_table(target, groups, depth):
    total = target.shape[0]
    hits = (target[:, None] == jnp.arange(groups, dtype=jnp.int32)[None, :]).astype(jnp.int32)
    before = jnp.cumsum(hits, axis=0) - hits
    ranking = jnp.sum(before * hits, axis=1)
    placed = target * depth + ranking
    match = placed[None, :] == jnp.arange(groups * depth, dtype=jnp.int32)[:, None]
    source = jnp.sum(jnp.where(match, jnp.arange(total, dtype=jnp.int32)[None, :], 0), axis=1)
    filled = jnp.any(match, axis=1)
    return (source, filled)


def phase_table(start, slope, first, channels):
    pixels = (jnp.arange(G, dtype=jnp.int32) - G // 2).astype(jnp.float32) * (2.0 * math.pi / G)
    angles = jnp.concatenate([pixels, pixels])
    shifts = jnp.concatenate(
        [jnp.zeros((G,), jnp.float32), jnp.full((G,), -0.5 * math.pi, jnp.float32)]
    )
    coarse = (first + 16 * jnp.arange(channels // 16, dtype=jnp.int32)).astype(jnp.float32)
    fine = jnp.arange(16, dtype=jnp.int32).astype(jnp.float32)
    centre = start[:, None] + coarse[None, :] * slope[:, None] - 0.5 * G
    outer = centre[:, :, None] * angles + shifts
    inner = (fine[None, :] * slope[:, None])[:, :, None] * angles
    table = (
        jnp.cos(outer)[:, :, None, :] * jnp.cos(inner)[:, None, :, :]
        - jnp.sin(outer)[:, :, None, :] * jnp.sin(inner)[:, None, :, :]
    )
    return table.reshape(start.shape[0], channels, 2 * G)


def grid_one(data, where, first):
    bound = data.shape[1]
    channels = data.shape[2]
    values = where.astype(jnp.float32)
    left = (
        phase_table(values[0], values[2], first, channels)
        .astype(jnp.bfloat16)
        .reshape(bound * channels, 2 * G)
    )
    right = phase_table(values[1], values[3], first, channels)
    signs = jnp.concatenate([-jnp.ones((G,), jnp.float32), jnp.ones((G,), jnp.float32)])
    swapped = jnp.roll(right, G, axis=2) * signs
    real_part = data[0].astype(jnp.float32)[:, :, None]
    imag_part = data[1].astype(jnp.float32)[:, :, None]
    weighted = (
        (real_part * right + imag_part * swapped)
        .astype(jnp.bfloat16)
        .reshape(bound * channels, 2 * G)
    )
    product = lax.dot_general(
        left, weighted, (((0,), (0,)), ((), ())), preferred_element_type=jnp.float32
    )
    return jnp.stack([product[:G, :G] - product[G:, G:], product[:G, G:] + product[G:, :G]])


def to_patch(image, weight):
    axis_values = (jnp.arange(G, dtype=jnp.int32) - G // 2).astype(jnp.float32) / (0.5 * G)
    radius = axis_values[:, None] ** 2 + axis_values[None, :] ** 2
    phase = math.pi * weight[:, None, None] * radius
    cosine, sine = (jnp.cos(phase), jnp.sin(phase))
    kernel_real = image[:, 0] * cosine - image[:, 1] * sine
    kernel_imag = image[:, 0] * sine + image[:, 1] * cosine
    index = jnp.arange(G, dtype=jnp.int32)
    turns = (index[:, None] * index[None, :] % G).astype(jnp.float32) * (2.0 * math.pi / G)
    table_real, table_imag = (jnp.cos(turns), -jnp.sin(turns))
    highest = lax.Precision.HIGHEST

    def from_left(matrix, field):
        return jnp.einsum("jl,slm->sjm", matrix, field, precision=highest)

    def from_right(field, matrix):
        return jnp.einsum("sjm,km->sjk", field, matrix, precision=highest)

    turned_real = from_left(table_real, kernel_real) - from_left(table_imag, kernel_imag)
    turned_imag = from_left(table_real, kernel_imag) + from_left(table_imag, kernel_real)
    patch_real = from_right(turned_real, table_real) - from_right(turned_imag, table_imag)
    patch_imag = from_right(turned_real, table_imag) + from_right(turned_imag, table_real)
    return jnp.stack([patch_real, patch_imag], axis=1) * (1.0 / G)


def per_device(visibilities, anchor, drift, target, subgrid_w, facet_owner, row_offset, col_offset):
    base_count = lax.axis_size("base")
    own_subgrids = subgrid_w.shape[0]
    all_subgrids = own_subgrids * base_count
    channels = visibilities.shape[2]
    first = lax.axis_index("freq") * channels
    source, filled = slot_table(target[:, 0], all_subgrids, CAP)
    picked = jnp.where(
        filled[None, :, None], jnp.take(visibilities, source, axis=1), jnp.zeros((), jnp.bfloat16)
    )
    slotted = picked.reshape(2, all_subgrids, CAP, channels)
    places = jnp.concatenate([anchor, drift], axis=0)
    located = jnp.where(
        filled[None, :], jnp.take(places, source, axis=1), jnp.zeros((), jnp.bfloat16)
    )
    located = located.reshape(4, all_subgrids, CAP)
    grid_data = jnp.moveaxis(slotted, 1, 0)
    grid_where = jnp.moveaxis(located, 1, 0)

    def single(item):
        return grid_one(item[0], item[1], first)

    images = lax.psum_scatter(
        lax.map(single, (grid_data, grid_where)), "base", scatter_dimension=0, tiled=True
    )
    images = lax.psum(images, "freq")
    patches = to_patch(images, subgrid_w)
    chosen, kept = slot_table(facet_owner[:, 0], base_count, FCAP)
    flattened = patches.reshape(own_subgrids, 2 * G * G)
    outgoing = jnp.where(kept[:, None], jnp.take(flattened, chosen, axis=0), 0.0)
    spots = jnp.stack([row_offset, col_offset], axis=1).astype(jnp.float32)
    sent_spots = jnp.where(kept[:, None], jnp.take(spots, chosen, axis=0), 0.0)
    arrived, arrived_spots = (
        lax.all_to_all(outgoing, "base", split_axis=0, concat_axis=0, tiled=True),
        lax.all_to_all(sent_spots, "base", split_axis=0, concat_axis=0, tiled=True),
    )
    corners = arrived_spots.astype(jnp.int32)

    def deposit(position, facet):
        start = (jnp.zeros((), jnp.int32), corners[position, 0], corners[position, 1])
        region = lax.dynamic_slice(facet, start, (2, G, G))
        patch = arrived[position].reshape(2, G, G)
        return lax.dynamic_update_slice(facet, region + patch, start)

    return lax.fori_loop(0, arrived.shape[0], deposit, jnp.zeros((2, FR, GY), jnp.float32))


def solution(mesh):
    return jax.shard_map(
        per_device,
        mesh=mesh,
        in_specs=(
            P(None, "base", "freq"),
            P(None, "base"),
            P(None, "base"),
            P("base", None),
            P("base"),
            P("base", None),
            P("base"),
            P("base"),
        ),
        out_specs=P(None, "base", None),
        check_vma=False,
    )
```

profile of v0, /device:TPU:1, one launch (start us, length us, event | category | flops | bytes accessed | tf_op | source)
XLA Modules:
  0.0 991.7 jit_solution(2251787866545427747)
XLA Ops:
  11.7 3.2 gather_fusion.1
  15.9 5.3 gather_fusion.2
  21.9 490.5 %while.26 = (s32[]{:T(128)}, f32[128,2,64,64]{3,2,1,0:T(8,128)}, bf16[128,4,8]{2,1,0:T(4,128)(2,1)S(1)}, s32[]{:T(128)}, bf16[128,2,8,256]{3,2,0,1:T(8,128)(2,1)...) while((s32[]{:T(128)}, f32[128,2,64,64]{3,2,1,0:T(8,128)}, bf16[128,4,8]{2,1,0:T(4,128)(2,1)S(1)}, ...), condition=%wide.region_10.11_spmd, body=%wide.region_9.10_spmd.sunk | while | flops 71423392 | bytes 5864877 | solution.py:118
  515.2 8.6 all-to-all-start
  524.1 75.4 %reduce-scatter.2.cloned.1.call-done = f32[8,2,64,64]{3,2,1,0:T(8,128)} async-done(((f32[128,2,64,64]{3,2,1,0:T(8,128)}), f32[8,2,64,64]{3,2,1,0:T(8,128)}) %reduce-scatter.2.cloned.1.call-update) | async-done | bytes 262160 | tf_op jit(solution)/shard_map/reduce_scatter | solution.py:117
  599.5 61.3 %all-reduce.2.cloned.1.call-done = f32[8,2,64,64]{3,2,1,0:T(8,128)} async-done(((f32[8,2,64,64]{3,2,1,0:T(8,128)}), f32[8,2,64,64]{3,2,1,0:T(8,128)}) %all-reduce.2.cloned.1.call-update) | async-done | bytes 262160 | tf_op jit(solution)/shard_map/psum | solution.py:120
  677.7 6.7 all-to-all-start.1
  684.7 14.0 %all-to-all-done.1 = f32[16,2,8192]{2,1,0:T(2,128)S(1)} async-done(((f32[16,2,8192]{2,1,0:T(2,128)}), f32[16,2,8192]{2,1,0:T(2,128)S(1)}, u32[]{:S(2)}, u32[]{:S(2)}) %all-to-all-start.1) | async-done | bytes 1048608 | tf_op jit(solution)/shard_map/all_to_all | solution.py:128
  699.4 8.1 broadcast_in_dim.170
  707.6 277.3 %while.27 = (s32[]{:T(128)}, f32[2,128,16384]{2,1,0:T(8,128)}, s32[32,2]{0,1:T(2,128)S(1)}, f32[32,8192]{1,0:T(8,128)S(1)}, s32[]{:T(128)}, /*index=5*/s32[]{:T(128)}, s32[]{:T(128)}, s32[]{:T(128)}) while((s32[]{:T(128)}, f32[2,128,16384]{2,1,0:T(8,128)}, s32[32,2]{0,1:T(2,128)S(1)}, f32[32,8192]{1,0:T(8,128)S(1)}, s32[]{:T(128)}, ...), condition=%wide.region_14.15_spmd, body=%wide.region_13.14_spmd.sunk | while | flops 8200 | bytes 295109 | solution.py:139
  713.2 3.0 dynamic_update_slice.19
  721.8 3.0 dynamic_update_slice.19
  730.4 3.0 dynamic_update_slice.19
  739.0 3.0 dynamic_update_slice.19
  747.6 3.2 dynamic_update_slice.19
  756.5 3.0 dynamic_update_slice.19
  782.3 3.3 dynamic_update_slice.19
  791.2 3.0 dynamic_update_slice.19
  834.2 3.2 dynamic_update_slice.19
  851.7 3.3 dynamic_update_slice.19
  869.1 3.2 dynamic_update_slice.19
  886.6 3.3 dynamic_update_slice.19
  921.3 3.0 dynamic_update_slice.19
  955.7 3.3 dynamic_update_slice.19
  (2275 shorter events, 622.9 us)
Async XLA Ops:
  6.5 9.4 copy-start
  6.5 15.3 %copy-start.6 = (f32[128]{0:T(128)S(1)}, f32[128]{0:T(128)}, u32[]{:S(2)}) copy-start(f32[128]{0:T(128)} %constant.174.clone.1) | copy-start | bytes 1540
  6.5 15.3 %copy-start.1 = (f32[128]{0:T(128)S(1)}, f32[128]{0:T(128)}, u32[]{:S(2)}) copy-start(f32[128]{0:T(128)} %constant.173.clone.1) | copy-start | bytes 1540
  6.5 592.9 %reduce-scatter.2.cloned.1.call-start = ((), (), s32[]{:S(2)}) async-start(), calls=%async_computation.3 | async-start | bytes 8912896 | tf_op jit(solution)/shard_map/reduce_scatter | solution.py:117
  512.3 0.7 copy-start.3
  512.3 0.7 copy-start.4
  512.3 0.8 copy-start.2
  512.3 87.2 %copy-start.5 = (f32[8]{0:T(128)S(1)}, f32[8]{0:T(128)}, u32[]{:S(2)}) copy-start(f32[8]{0:T(128)} %param.16) | copy-start | bytes 100
  515.2 162.5 %all-to-all-start = ((f32[16,2,2]{1,2,0:T(2,128)}), f32[16,2,2]{1,2,0:T(2,128)S(1)}, u32[]{:S(2)}, u32[]{:S(2)}) async-start(f32[16,2,2]{1,2,0:T(2,128)} %copy.84), calls=%async_computation | async-start | bytes 32768 | tf_op jit(solution)/shard_map/all_to_all | solution.py:129
  523.8 137.0 %all-reduce.2.cloned.1.call-start = ((), (), s32[]{:S(2)}) async-start(), calls=%async_computation.4 | async-start | bytes 1048576 | tf_op jit(solution)/shard_map/psum | solution.py:120
  677.7 21.0 %all-to-all-start.1 = ((f32[16,2,8192]{2,1,0:T(2,128)}), f32[16,2,8192]{2,1,0:T(2,128)S(1)}, u32[]{:S(2)}, u32[]{:S(2)}) async-start(f32[16,2,8192]{2,1,0:T(2,128)} %select_select_fusion), calls=%async_computation.2 | async-start | bytes 2097152 | tf_op jit(solution)/shard_map/all_to_all | solution.py:128
Sparse Core Ops, SparseCore 0:
  512.5 86.9 reduce-scatter.1
  601.8 58.9 all-reduce.1
where the time goes:
time: 1010 us; the launch traced here: 992 us
  other arithmetic  298 us (30%)
  local copies, waits for them, and re-layouts  214 us (21%)
  matrix products  171 us (17%)
  waiting for transfers between devices  151 us (15%)
  loops' own time  129 us (13%)
  starting transfers between devices  15.5 us (2%)
  between operations  13.7 us (1%)
    dot_general x128, matrix products, grid_one(): lax.dot_general(left, weighted, (((0,), (0,)), ((), ())), preferred_eleme...  158 us
    cos x128, other arithmetic, phase_table(): jnp.cos(outer)[:, :, None, :] * jnp.cos(inner)[:, None, :, :]  126 us
    another operation x1, loops' own time, per_device(): lax.fori_loop(0, arrived.shape[0], deposit, jnp.zeros((2, FR, GY), jnp.fl...  120 us
    dynamic_update_slice x32, local copies, waits for them, and re-layouts, deposit(): return lax.dynamic_update_slice(facet, region + patch, start)  98.1 us
    dynamic_update_slice x128, other arithmetic, per_device(): lax.map(single, (grid_data, grid_where))  82.3 us
    reduce_scatter x1, waiting for transfers between devices, per_device(): lax.psum_scatter(lax.map(single, (grid_data, grid_where)), 'base', scatte...  75.4 us
    psum x1, waiting for transfers between devices, per_device(): images = lax.psum(images, 'freq')  61.3 us
    slice x128, local copies, waits for them, and re-layouts, grid_one(): swapped = jnp.roll(right, G, axis=2) * signs  44.2 us
  transfers between devices with their start and end apart: 4, of which 3 were waited for; matrix products, arithmetic and copies ran while one was open for 2% of the time, Pallas kernels for 0%

commit v1 on v0

v1 whole, which is shorter than its diff:
```python
import functools
import math

import jax
import jax.numpy as jnp
import numpy as np
from jax import lax
from jax.experimental import pallas as pl
from jax.experimental.pallas import tpu as pltpu
from jax.sharding import PartitionSpec as P

G = 64
GY = 16384
CAP = 8
FCAP = 2
FR = 128
NT = (((1,), (1,)), ((), ()))
F32 = jnp.float32
BF16 = jnp.bfloat16
VMEM = pltpu.MemorySpace.VMEM
SMEM = pltpu.MemorySpace.SMEM


def vmem():
    return pl.BlockSpec(memory_space=VMEM)


def smem():
    return pl.BlockSpec(memory_space=SMEM)


def prep_kernel(target_ref, vis_ref, anchor_ref, drift_ref, vr_ref, vi_ref, co_ref):
    blocks = target_ref.shape[1]
    groups = blocks // CAP
    target = target_ref[...]
    hits = (lax.broadcasted_iota(jnp.int32, (groups, blocks), 0) == target).astype(F32)
    earlier = lax.broadcasted_iota(jnp.int32, (blocks, blocks), 0) < lax.broadcasted_iota(
        jnp.int32, (blocks, blocks), 1
    )
    before = jnp.dot(hits.astype(BF16), earlier.astype(F32).astype(BF16), preferred_element_type=F32)
    ranking = jnp.sum(before * hits, axis=0, keepdims=True)
    placed = target * CAP + ranking.astype(jnp.int32)
    step = 128

    def chunk(i, carry):
        start = pl.multiple_of(i * step, step)
        rows = pl.ds(start, step)
        match = lax.broadcasted_iota(jnp.int32, (step, blocks), 0) + start == placed
        pick = match.astype(F32).astype(BF16)
        vr_ref[rows, :] = jnp.dot(pick, vis_ref[0], preferred_element_type=F32)
        vi_ref[rows, :] = jnp.dot(pick, vis_ref[1], preferred_element_type=F32)
        co_ref[rows, 0:2] = lax.dot_general(pick, anchor_ref[...], NT, preferred_element_type=F32)
        co_ref[rows, 2:4] = lax.dot_general(pick, drift_ref[...], NT, preferred_element_type=F32)
        return carry

    lax.fori_loop(0, blocks // step, chunk, 0)


def prep(target, visibilities, anchor, drift):
    _, blocks, channels = visibilities.shape
    return pl.pallas_call(
        prep_kernel,
        out_shape=(
            jax.ShapeDtypeStruct((blocks, channels), F32),
            jax.ShapeDtypeStruct((blocks, channels), F32),
            jax.ShapeDtypeStruct((blocks, 4), F32),
        ),
        in_specs=[vmem()] * 4,
        out_specs=(vmem(), vmem(), vmem()),
        compiler_params=pltpu.CompilerParams(vmem_limit_bytes=48 << 20),
        name="prep",
    )(target.reshape(1, blocks), visibilities, anchor, drift)


def trig(h):
    z = h * h
    s = 1 / 362880 + z * (-1 / 39916800)
    s = h * (1.0 + z * (-1 / 6 + z * (1 / 120 + z * (-1 / 5040 + z * s))))
    c = -1 / 3628800 + z * (1 / 479001600)
    c = 1.0 + z * (-0.5 + z * (1 / 24 + z * (-1 / 720 + z * (1 / 40320 + z * c))))
    return c, s


HALF = 152


def put(tab, row, v):
    tab[row : row + 8, :] = v[:, :128]
    tab[HALF + row : HALF + row + 8, :] = v[:, 128:]


def base_rows(h, tab):
    c0, s0 = trig(h)
    k1 = 4.0 * c0 * c0 - 2.0
    k2 = k1 * k1 - 2.0
    k4 = k2 * k2 - 2.0
    k8 = k4 * k4 - 2.0
    s8 = (2.0 * s0 * c0) * k1 * k2 * k4
    cp, cc = c0, (k1 - 1.0) * c0
    sp, sc = s0, (k1 + 1.0) * s0
    put(tab, 0, c0)
    put(tab, 64, s0)
    for p in range(1, 8):
        put(tab, 8 * p, cc)
        put(tab, 64 + 8 * p, sc)
        cp, cc = cc, k1 * cc - cp
        sp, sc = sc, k1 * sc - sp
    put(tab, 128, k8)
    put(tab, 136, 0.5 * k8)
    put(tab, 144, s8)
    return c0, s0


def expand(tab, s, h):
    o = HALF * h
    k8 = tab[o + 128 + s : o + 129 + s, :]
    c8 = tab[o + 136 + s : o + 137 + s, :]
    s8 = tab[o + 144 + s : o + 145 + s, :]
    a0 = tab[pl.ds(o + s, 8, stride=8), :]
    b0 = tab[pl.ds(o + 64 + s, 8, stride=8), :]
    a1 = c8 * a0 - s8 * b0
    b1 = c8 * b0 + s8 * a0
    a2 = k8 * a1 - a0
    b2 = k8 * b1 - b0
    a3 = k8 * a2 - a1
    b3 = k8 * b2 - b1
    return jnp.concatenate([a0, a1, a2, a3, b0, b1, b2, b3], axis=0)


def one_subgrid(g, chan, vr_ref, vi_ref, co_ref, tx, ty, tv):
    rows = pl.ds(pl.multiple_of(8 * g, 8), 8)
    co = co_ref[rows, :]
    hx = (co[:, 0:1] - 0.5 * G + chan * co[:, 2:3]) * (math.pi / G)
    hy = (co[:, 1:2] - 0.5 * G + chan * co[:, 3:4]) * (math.pi / G)
    cx, sx = base_rows(hx, tx)
    cy, sy = base_rows(hy, ty)
    er = cx * cy - sx * sy
    ei = cx * sy + sx * cy
    vr = vr_ref[rows, :]
    vi = vi_ref[rows, :]
    tv[0:8, :] = vr * er + vi * ei
    tv[8:16, :] = vi * er - vr * ei
    acc = None
    for s in range(8):
        f = jnp.concatenate([expand(tx, s, h).astype(BF16) for h in (0, 1)], axis=1)
        parts = []
        for h in (0, 1):
            g0 = expand(ty, s, h)
            cut = slice(128 * h, 128 * h + 128)
            both = [g0 * tv[s : s + 1, cut], g0 * tv[8 + s : 9 + s, cut]]
            parts.append(jnp.concatenate(both, axis=0).astype(BF16))
        r = jnp.concatenate(parts, axis=1)
        d = lax.dot_general(f, r, NT, preferred_element_type=F32)
        acc = d if acc is None else acc + d
    return acc


def grid_kernel(first_ref, vr_ref, vi_ref, co_ref, out_ref, tx, ty, tv):
    chan = (lax.broadcasted_iota(jnp.int32, (8, 256), 1) + first_ref[0]).astype(F32)

    def body(g, carry):
        out_ref[g] = one_subgrid(g, chan, vr_ref, vi_ref, co_ref, tx, ty, tv)
        return carry

    lax.fori_loop(0, out_ref.shape[0], body, 0)


def grid_all(first, vr, vi, co):
    return pl.pallas_call(
        grid_kernel,
        out_shape=jax.ShapeDtypeStruct((vr.shape[0] // CAP, G, 2 * G), F32),
        in_specs=[smem()] + [vmem()] * 3,
        out_specs=vmem(),
        scratch_shapes=[
            pltpu.VMEM((2 * HALF, 128), F32),
            pltpu.VMEM((2 * HALF, 128), F32),
            pltpu.VMEM((16, 256), F32),
        ],
        compiler_params=pltpu.CompilerParams(vmem_limit_bytes=48 << 20),
        name="gridding",
    )(first, vr, vi, co)


def constants():
    l = np.arange(G) - G // 2 + 0.5
    p = np.arange(G // 2) + 0.5
    same = (np.abs(l)[:, None] == p[None, :]).astype(np.float64)
    a = np.concatenate([same, 0 * same], axis=1)
    b = np.concatenate([0 * same, same * np.sign(l)[:, None]], axis=1)
    turns = 2 * np.pi * ((np.arange(G)[:, None] * np.arange(G)[None, :]) % G) / G
    fr, fi = np.cos(turns), -np.sin(turns)
    left1 = np.concatenate([a, b], axis=0)
    right1 = np.block([[a.T, b.T], [-b.T, a.T]])
    left2 = np.concatenate([fr, fi], axis=0)
    right2 = np.block([[fr, fi], [-fi, fr]]) / G
    return [x.astype(np.float32) for x in (left1, right1, left2, right2)]


def dot32(a, b):
    return jnp.dot(a, b, precision=lax.Precision.HIGHEST, preferred_element_type=F32)


def make_patch(m, w, left1, right1, left2, right2):
    lane = lax.broadcasted_iota(jnp.int32, (G, 2 * G), 1)
    sign = jnp.where(lane < G, -1.0, 1.0).astype(F32)
    row = lax.broadcasted_iota(jnp.int32, (G, 2 * G), 0)
    xl = (row - G // 2).astype(F32) * (2.0 / G)
    xm = (lane % G - G // 2).astype(F32) * (2.0 / G)
    c, s = trig((0.25 * math.pi) * w * (xl * xl + xm * xm))
    for _ in range(2):
        c, s = 2.0 * c * c - 1.0, 2.0 * c * s
    both = dot32(left1, m)
    y = both[:G] + sign * jnp.roll(both[G:], G, axis=1)
    z = dot32(y, right1)
    k = z * c + jnp.roll(z, G, axis=1) * (s * sign)
    both = dot32(left2, k)
    y = both[:G] + sign * jnp.roll(both[G:], G, axis=1)
    return dot32(y, right2)


def deposit_kernel(me_ref, owner_ref, row_ref, col_ref, slot_ref, out_ref, acc, sem):
    me = me_ref[0]
    zeros = jnp.zeros((8, 2048), F32)

    def clear(i, carry):
        q = i // (FR // 8)
        r = pl.ds(pl.multiple_of((i % (FR // 8)) * 8, 8), 8)
        for j in range(GY // 2048):
            acc[q, r, 2048 * j : 2048 * (j + 1)] = zeros
        return carry

    lax.fori_loop(0, 2 * FR // 8, clear, 0)
    for q in range(2):
        for j in range(GY // 2048):
            acc[q, FR : FR + 8, 2048 * j : 2048 * (j + 1)] = zeros
    lane = lax.broadcasted_iota(jnp.int32, (G + 8, 128), 1)

    def place(index, slot):
        row = row_ref[index]
        r = pl.ds(pl.multiple_of(row // 8 * 8, 8), G + 8)
        col = col_ref[index]
        tile = col // 128
        c = col % 128
        first = pl.ds(pl.multiple_of(tile * 128, 128), 128)
        second = pl.ds(pl.multiple_of(jnp.minimum(tile + 1, GY // 128 - 1) * 128, 128), 128)
        patch = jnp.concatenate([slot_ref[slot], jnp.zeros((8, 2 * G), F32)], axis=0)
        patch = pltpu.roll(patch, row % 8, 0)
        for q in range(2):
            part = jnp.where(lane < G, patch if q == 0 else pltpu.roll(patch, G, 1), 0.0)
            moved = pltpu.roll(part, c, 1)
            acc[q, r, first] += jnp.where(lane >= c, moved, 0.0)
            acc[q, r, second] += jnp.where(lane < c, moved, 0.0)

    own = CAP

    def source(b, carry):
        seen = jnp.int32(0)
        for s in range(own):
            index = b * own + s
            mine = owner_ref[index] == me

            @pl.when(mine)
            def _():
                place(index, seen * 16 + b)

            seen = seen + mine.astype(jnp.int32)
        return carry

    lax.fori_loop(0, 16, source, 0)
    copies = []
    for q in range(2):
        for j in range(8):
            r = pl.ds(j * 16, 16)
            copies.append(pltpu.make_async_copy(acc.at[q, r], out_ref.at[q, r], sem.at[q * 8 + j]))
    for copy in copies:
        copy.start()
    for copy in copies:
        copy.wait()


def deposit(me, owners, rows, cols, slots):
    return pl.pallas_call(
        deposit_kernel,
        out_shape=jax.ShapeDtypeStruct((2, FR, GY), F32),
        in_specs=[smem()] * 4 + [vmem()],
        out_specs=pl.BlockSpec(memory_space=pl.ANY),
        scratch_shapes=[pltpu.VMEM((2, FR + 8, GY), F32), pltpu.SemaphoreType.DMA((16,))],
        compiler_params=pltpu.CompilerParams(vmem_limit_bytes=48 << 20),
        name="deposit",
    )(me, owners, rows, cols, slots)


def slot_table(target, groups, depth):
    total = target.shape[0]
    hits = (target[:, None] == jnp.arange(groups, dtype=jnp.int32)[None, :]).astype(jnp.int32)
    before = jnp.cumsum(hits, axis=0) - hits
    ranking = jnp.sum(before * hits, axis=1)
    placed = target * depth + ranking
    match = placed[None, :] == jnp.arange(groups * depth, dtype=jnp.int32)[:, None]
    source = jnp.sum(jnp.where(match, jnp.arange(total, dtype=jnp.int32)[None, :], 0), axis=1)
    return source


def per_device(visibilities, anchor, drift, target, subgrid_w, facet_owner, row_offset, col_offset):
    base_count = lax.axis_size("base")
    own = subgrid_w.shape[0]
    first = (lax.axis_index("freq") * visibilities.shape[2]).astype(jnp.int32).reshape(1)
    me = lax.axis_index("base").astype(jnp.int32).reshape(1)
    vr, vi, co = prep(target, visibilities, anchor, drift)
    table = jnp.stack([facet_owner[:, 0], row_offset, col_offset])
    table = lax.all_gather(table, "base", axis=1, tiled=True)
    images = grid_all(first, vr, vi, co)
    images = lax.psum_scatter(images, "base", scatter_dimension=0, tiled=True)
    images = lax.psum(images, "freq")
    consts = [jnp.asarray(x) for x in constants()]
    patches = jax.vmap(lambda m, w: make_patch(m, w, *consts))(images, subgrid_w)
    chosen = slot_table(facet_owner[:, 0], base_count, FCAP)
    outgoing = jnp.take(patches, chosen, axis=0).reshape(base_count, FCAP, G, 2 * G)
    arrived = lax.all_to_all(outgoing, "base", split_axis=0, concat_axis=0, tiled=True)
    slots = jnp.moveaxis(arrived, 1, 0).reshape(FCAP * base_count, G, 2 * G)
    return deposit(me, table[0], table[1], table[2], slots)


def solution(mesh):
    return jax.shard_map(
        per_device,
        mesh=mesh,
        in_specs=(
            P(None, "base", "freq"),
            P(None, "base"),
            P(None, "base"),
            P("base", None),
            P("base"),
            P("base", None),
            P("base"),
            P("base"),
        ),
        out_specs=P(None, "base", None),
        check_vma=False,
    )
```

time: 1010 us -> 280 us (0.28)
  the two profiles are of different devices: /device:TPU:1 before, /device:TPU:22 now
where the time goes in v1:
time: 280 us; the launch traced here: 279 us
  waiting for transfers between devices  136 us (49%)
  Pallas kernels  77.2 us (28%)
  blocking collectives  31.4 us (11%)
  between operations  13.6 us (5%)
  starting transfers between devices  7.45 us (3%)
  matrix products  4.99 us (2%)
  local copies, waits for them, and re-layouts  4.59 us (2%)
  other arithmetic  4.23 us (2%)
    reduce_scatter x1, waiting for transfers between devices, per_device(): images = lax.psum_scatter(images, 'base', scatter_dimension=0, tiled=True)  76.5 us
    psum x1, waiting for transfers between devices, per_device(): images = lax.psum(images, 'freq')  59.5 us
    pallas_call x1, Pallas kernels, grid_all(): pl.pallas_call(grid_kernel, out_shape=jax.ShapeDtypeStruct((vr.shape[0] /...  57.9 us
    all_gather x1, blocking collectives, per_device(): table = lax.all_gather(table, 'base', axis=1, tiled=True)  31.4 us
    pallas_call x1, Pallas kernels, deposit(): pl.pallas_call(deposit_kernel, out_shape=jax.ShapeDtypeStruct((2, FR, GY)...  14.6 us
    all_to_all x1, starting transfers between devices, per_device(): lax.all_to_all(outgoing, 'base', split_axis=0, concat_axis=0, tiled=True)  7.4 us
  transfers between devices with their start and end apart: 3, of which 2 were waited for; matrix products, arithmetic and copies ran while one was open for 1% of the time, Pallas kernels for 0%

profile of v1, /device:TPU:22, one launch (start us, length us, event | category | flops | bytes accessed | tf_op | source)
XLA Modules:
  0.0 279.4 jit_solution(13066335755431227631)
XLA Ops:
  6.5 1.3 copy-done
  7.8 0.7 copy-done.1
  8.5 0.7 copy-done.2
  9.2 0.7 copy-done.3
  9.9 4.6 %prep.1 = (f32[1024,256]{1,0:T(8,128)S(1)}, f32[1024,256]{1,0:T(8,128)S(1)}, f32[1024,4]{1,0:T(8,128)S(1)}) custom-call(s32[1,1024]{1,0:T(1,128)S(1)} %bitcast.56, bf16[2,1024,256]{2,1,0:T(8,128)(2,1)S(1)} %copy-done, bf16[2,1024]{1,0:T(2,128)(2,1)S(1)} %copy-done.2, bf16[2,1024]{1,0:T(2,128)(2,1)S(1)} %copy-done.3), custom_call_target="tpu_custom_call" | custom-call | tf_op jit(solution)/shard_map/prep/pallas_call | solution.py:61
  14.5 57.9 %gridding.1 = f32[128,64,128]{2,1,0:T(8,128)} custom-call(s32[1]{0:T(128)} %bitcast.13.first_ref, f32[1024,256]{1,0:T(8,128)S(1)} %get-tuple-element.8.vr_ref, f32[1024,256]{1,0:T(8,128)S(1)} %get-tuple-element.9.vi_ref, f32[1024,4]{1,0:T(8,128)S(1)} %get-tuple-element.10.co_ref), custom_call_target="tpu_custom_call" | custom-call | tf_op jit(solution)/shard_map/gridding/pallas_call | solution.py:169
  72.5 0.7 fusion.64
  73.2 0.8 select_reduce_fusion.1
  74.1 0.7 multiply_add_fusion.1
  74.9 0.7 broadcast_multiply_fusion
  75.7 76.5 %reduce-scatter.2.cloned.1.call-done = f32[8,64,128]{2,1,0:T(8,128)} async-done(((f32[128,64,128]{2,1,0:T(8,128)}), f32[8,64,128]{2,1,0:T(8,128)}) %reduce-scatter.2.cloned.1.call-update) | async-done | bytes 262160 | tf_op jit(solution)/shard_map/reduce_scatter | solution.py:313
  152.2 59.5 %all-reduce.2.cloned.1.call-done = f32[8,64,128]{2,1,0:T(8,128)} async-done(((f32[8,64,128]{2,1,0:T(8,128)}), f32[8,64,128]{2,1,0:T(8,128)}) %all-reduce.2.cloned.1.call-update) | async-done | bytes 262160 | tf_op jit(solution)/shard_map/psum | solution.py:314
  211.7 1.6 fusion.84
  213.3 0.1 slice_bitcast_fusion.4
  213.4 1.3 fusion.36
  214.7 0.1 fusion.83
  214.9 1.7 fusion.26
  216.6 0.1 slice_bitcast_fusion.1
  216.7 0.4 fusion.33
  217.2 0.6 gather_fusion
  217.8 1.1 broadcast_select_fusion
  218.9 7.4 %all-to-all-start = ((f32[16,2,64,128]{3,2,1,0:T(8,128)}), f32[16,2,64,128]{3,2,1,0:T(8,128)S(1)}, u32[]{:S(2)}, u32[]{:S(2)}) async-start(f32[16,2,64,128]{3,2,1,0:T(8,128)} %broadcast_select_fusion), calls=%async_computation.1 | async-start | bytes 2097152 | tf_op jit(solution)/shard_map/all_to_all | solution.py:319
  226.3 31.4 %all-gather = s32[16,8,3]{1,2,0:T(4,128)S(1)} all-gather(s32[1,8,3]{1,2,0:T(4,128)S(1)} %add_bitcast_fusion), channel_id=1, replica_groups=mesh['base'=16,'freq'=8] {'base'}, dimensions={0}, use_global_device_ids=true | all-gather | bytes 1632 | tf_op jit(solution)/shard_map/all_gather | solution.py:311
  257.9 14.6 %deposit.1 = f32[2,128,16384]{2,1,0:T(8,128)} custom-call(s32[1]{0:T(128)} %bitcast.me_ref, s32[128]{0:T(128)S(1)} %get-tuple-element.19.owner_ref, s32[128]{0:T(128)S(1)} %get-tuple-element.18.row_ref, s32[128]{0:T(128)S(1)} %get-tuple-element.17.col_ref, f32[32,64,128]{2,1,0:T(8,128)S(1)} %bitcast.55), custom_call_target="tpu_custom_call" | custom-call | tf_op jit(solution)/shard_map/deposit/pallas_call | solution.py:282
  (33 shorter events, 0.6 us)
Async XLA Ops:
  6.5 219.8 %copy-start.5 = (s32[8,1]{0,1:T(1,128)S(1)}, s32[8,1]{0,1:T(1,128)}, u32[]{:S(2)}) copy-start(s32[8,1]{0,1:T(1,128)} %param.17) | copy-start | bytes 100
  6.5 219.8 %copy-start.6 = (s32[8]{0:T(128)S(1)}, s32[8]{0:T(128)}, u32[]{:S(2)}) copy-start(s32[8]{0:T(128)} %param.19) | copy-start | bytes 100
  6.5 219.8 %copy-start.7 = (s32[8]{0:T(128)S(1)}, s32[8]{0:T(128)}, u32[]{:S(2)}) copy-start(s32[8]{0:T(128)} %param.18) | copy-start | bytes 100
  6.5 145.6 %reduce-scatter.2.cloned.1.call-start = ((), (), s32[]{:S(2)}) async-start(), calls=%async_computation.2 | async-start | bytes 4456448 | tf_op jit(solution)/shard_map/reduce_scatter | solution.py:313
  6.5 1.3 copy-start
  7.8 0.7 copy-start.1
  8.5 0.7 copy-start.2
  9.2 0.7 copy-start.3
  9.9 206.8 %copy-start.4 = (f32[128,128,1]{1,0,2:T(8,128)S(1)}, f32[128,128,1]{1,0,2:T(8,128)}, u32[]{:S(2)}) copy-start(f32[128,128,1]{1,0,2:T(8,128)} %constant.108) | copy-start | bytes 196612
  72.4 139.3 %all-reduce.2.cloned.1.call-start = ((), (), s32[]{:S(2)}) async-start(), calls=%async_computation.3 | async-start | bytes 524288 | tf_op jit(solution)/shard_map/psum | solution.py:314
  218.9 39.0 %all-to-all-start = ((f32[16,2,64,128]{3,2,1,0:T(8,128)}), f32[16,2,64,128]{3,2,1,0:T(8,128)S(1)}, u32[]{:S(2)}, u32[]{:S(2)}) async-start(f32[16,2,64,128]{3,2,1,0:T(8,128)} %broadcast_select_fusion), calls=%async_computation.1 | async-start | bytes 2097152 | tf_op jit(solution)/shard_map/all_to_all | solution.py:319
Sparse Core Ops, SparseCore 0:
  72.6 79.5 reduce-scatter.1
  154.6 57.0 all-reduce.1

commit v2 on v1

--- a/solution.py
+++ b/solution.py
@@ -155,32 +155,6 @@
     return acc
 
 
-def grid_kernel(first_ref, vr_ref, vi_ref, co_ref, out_ref, tx, ty, tv):
-    chan = (lax.broadcasted_iota(jnp.int32, (8, 256), 1) + first_ref[0]).astype(F32)
-
-    def body(g, carry):
-        out_ref[g] = one_subgrid(g, chan, vr_ref, vi_ref, co_ref, tx, ty, tv)
-        return carry
-
-    lax.fori_loop(0, out_ref.shape[0], body, 0)
-
-
-def grid_all(first, vr, vi, co):
-    return pl.pallas_call(
-        grid_kernel,
-        out_shape=jax.ShapeDtypeStruct((vr.shape[0] // CAP, G, 2 * G), F32),
-        in_specs=[smem()] + [vmem()] * 3,
-        out_specs=vmem(),
-        scratch_shapes=[
-            pltpu.VMEM((2 * HALF, 128), F32),
-            pltpu.VMEM((2 * HALF, 128), F32),
-            pltpu.VMEM((16, 256), F32),
-        ],
-        compiler_params=pltpu.CompilerParams(vmem_limit_bytes=48 << 20),
-        name="gridding",
-    )(first, vr, vi, co)
-
-
 def constants():
     l = np.arange(G) - G // 2 + 0.5
     p = np.arange(G // 2) + 0.5
@@ -196,6 +170,10 @@
     return [x.astype(np.float32) for x in (left1, right1, left2, right2)]
 
 
+def swap(x):
+    return pltpu.roll(x, G, 1)
+
+
 def dot32(a, b):
     return jnp.dot(a, b, precision=lax.Precision.HIGHEST, preferred_element_type=F32)
 
@@ -210,15 +188,231 @@
     for _ in range(2):
         c, s = 2.0 * c * c - 1.0, 2.0 * c * s
     both = dot32(left1, m)
-    y = both[:G] + sign * jnp.roll(both[G:], G, axis=1)
+    y = both[:G] + sign * swap(both[G:])
     z = dot32(y, right1)
-    k = z * c + jnp.roll(z, G, axis=1) * (s * sign)
+    k = z * c + swap(z) * (s * sign)
     both = dot32(left2, k)
-    y = both[:G] + sign * jnp.roll(both[G:], G, axis=1)
+    y = both[:G] + sign * swap(both[G:])
     return dot32(y, right2)
 
 
-def deposit_kernel(me_ref, owner_ref, row_ref, col_ref, slot_ref, out_ref, acc, sem):
+MESH = pl.DeviceIdType.MESH
+
+
+def main_kernel(
+    nb,
+    nf,
+    owner_ref,
+    w_ref,
+    spot_ref,
+    vr_ref,
+    vi_ref,
+    co_ref,
+    left1,
+    right1,
+    left2,
+    right2,
+    slots,
+    table,
+    tx,
+    ty,
+    tv,
+    send,
+    recv,
+    total,
+    fsum,
+    gath,
+    outb,
+    spot_s,
+    spot_r,
+    base_s,
+    base_r,
+    freq_s,
+    freq_r,
+    gath_s,
+    gath_r,
+    out_s,
+    out_r,
+    pair_s,
+    pair_r,
+):
+    me_b = lax.axis_index("base")
+    me_f = lax.axis_index("freq")
+    own = total.shape[0]
+    core = me_f % 2
+
+    def base_copy(src, dst, ss, rs, t):
+        return pltpu.make_async_remote_copy(
+            src_ref=src, dst_ref=dst, send_sem=ss, recv_sem=rs, device_id={"base": (me_b + t) % nb}, device_id_type=MESH
+        )
+
+    def freq_copy(src, dst, ss, rs, d):
+        return pltpu.make_async_remote_copy(
+            src_ref=src, dst_ref=dst, send_sem=ss, recv_sem=rs, device_id={"freq": (me_f + d) % nf}, device_id_type=MESH
+        )
+
+    def each(low, high, body):
+        def step(i, carry):
+            body(i)
+            return carry
+
+        lax.fori_loop(low, high, step, 0)
+
+    barrier = pltpu.get_barrier_semaphore()
+    each(1, nb, lambda t: pl.semaphore_signal(barrier, inc=1, device_id={"base": (me_b + t) % nb}, device_id_type=MESH))
+    each(1, nf, lambda d: pl.semaphore_signal(barrier, inc=1, device_id={"freq": (me_f + d) % nf}, device_id_type=MESH))
+    pl.semaphore_wait(barrier, nb + nf - 2)
+
+    def spot_copy(t):
+        return base_copy(spot_ref, table.at[pl.ds(me_b, 1)], spot_s.at[t - 1], spot_r.at[t - 1], t)
+
+    each(1, nb, lambda t: spot_copy(t).start())
+    table[pl.ds(me_b, 1), :] = spot_ref[...]
+
+    channels = vr_ref.shape[1]
+    chan = (lax.broadcasted_iota(jnp.int32, (8, channels), 1) + me_f * channels).astype(F32)
+
+    def share_copy(t):
+        return base_copy(send.at[t], recv.at[t], base_s.at[t], base_r.at[t], t + 1)
+
+    def group(t):
+        owner = (me_b + 1 + t) % nb
+
+        def one(j):
+            g = owner * own + j
+            send[t, j] = one_subgrid(g, chan, vr_ref, vi_ref, co_ref, tx, ty, tv).astype(BF16)
+
+        each(0, own, one)
+
+        @pl.when(t < nb - 1)
+        def _():
+            share_copy(t).start()
+
+    each(0, nb, group)
+
+    def own_share(j):
+        total[j] = send[nb - 1, j].astype(F32)
+
+    each(0, own, own_share)
+
+    def add_share(t):
+        share_copy(t).wait_recv()
+
+        def add(j):
+            total[j] += recv[t, j].astype(F32)
+
+        each(0, own, add)
+
+    each(0, nb - 1, add_share)
+
+    def sum_copy(d):
+        return freq_copy(total.at[(me_f + d) % nf], fsum.at[d - 1], freq_s.at[d - 1], freq_r.at[d - 1], d)
+
+    each(1, nf, lambda d: sum_copy(d).start())
+    m = total[me_f]
+    for d in range(1, nf):
+        sum_copy(d).wait_recv()
+        m = m + fsum[d - 1]
+    gath[me_f] = make_patch(m, w_ref[me_f], left1[...], right1[...], left2[...], right2[...])
+
+    def gath_copy(d):
+        return freq_copy(gath.at[me_f], gath.at[me_f], gath_s.at[d - 1], gath_r.at[d - 1], d)
+
+    each(1, nf, lambda d: gath_copy(d).start())
+    each(1, nf, lambda d: gath_copy(d).wait_recv())
+
+    def out_copy(t):
+        return base_copy(outb.at[(me_b + t) % nb], slots.at[core, me_b], out_s.at[t - 1], out_r.at[t - 1], t)
+
+    def pick(o):
+        seen = jnp.int32(0)
+        index = jnp.int32(0)
+        for s in range(own):
+            hit = (owner_ref[s] == o).astype(jnp.int32)
+            use = hit * (seen == core).astype(jnp.int32)
+            index = index + use * s
+            seen = seen + hit
+        return gath[index]
+
+    def ship(t):
+        o = (me_b + t) % nb
+        outb[o] = pick(o)
+        out_copy(t).start()
+
+    each(1, nb, ship)
+    slots[core, me_b] = pick(me_b)
+
+    def pair_copy(t):
+        source = (me_b + nb - t) % nb
+        part = slots.at[core, source]
+        return pltpu.make_async_remote_copy(
+            src_ref=part,
+            dst_ref=part,
+            send_sem=pair_s.at[t],
+            recv_sem=pair_r.at[t],
+            device_id={"freq": me_f + 1 - 2 * core},
+            device_id_type=MESH,
+        )
+
+    pair_copy(0).start()
+
+    def forward(t):
+        out_copy(t).wait_recv()
+        pair_copy(t).start()
+
+    each(1, nb, forward)
+    each(0, nb, lambda t: pair_copy(t).wait())
+    each(1, nb, lambda t: out_copy(t).wait_send())
+    each(1, nf, lambda d: gath_copy(d).wait_send())
+    each(1, nf, lambda d: sum_copy(d).wait_send())
+    each(0, nb - 1, lambda t: share_copy(t).wait_send())
+    each(1, nb, lambda t: spot_copy(t).wait())
+
+
+def main(owner, w, spot, vr, vi, co, nb, nf):
+    own = w.shape[0]
+    unit = (G, 2 * G)
+    dma = pltpu.SemaphoreType.DMA
+    consts = [jnp.asarray(x) for x in constants()]
+    return pl.pallas_call(
+        functools.partial(main_kernel, nb, nf),
+        out_shape=(
+            jax.ShapeDtypeStruct((FCAP, nb) + unit, F32),
+            jax.ShapeDtypeStruct((nb, 128), jnp.int32),
+        ),
+        in_specs=[smem()] * 2 + [vmem()] * 8,
+        out_specs=(vmem(), vmem()),
+        scratch_shapes=[
+            pltpu.VMEM((2 * HALF, 128), F32),
+            pltpu.VMEM((2 * HALF, 128), F32),
+            pltpu.VMEM((16, 256), F32),
+            pltpu.VMEM((nb, own) + unit, BF16),
+            pltpu.VMEM((nb - 1, own) + unit, BF16),
+            pltpu.VMEM((own,) + unit, F32),
+            pltpu.VMEM((nf - 1,) + unit, F32),
+            pltpu.VMEM((nf,) + unit, F32),
+            pltpu.VMEM((nb,) + unit, F32),
+            dma((nb - 1,)),
+            dma((nb - 1,)),
+            dma((nb - 1,)),
+            dma((nb - 1,)),
+            dma((nf - 1,)),
+            dma((nf - 1,)),
+            dma((nf - 1,)),
+            dma((nf - 1,)),
+            dma((nb - 1,)),
+            dma((nb - 1,)),
+            dma((nb,)),
+            dma((nb,)),
+        ],
+        compiler_params=pltpu.CompilerParams(
+            vmem_limit_bytes=48 << 20, collective_id=0, has_side_effects=True
+        ),
+        name="main",
+    )(owner, w, spot, vr, vi, co, *consts)
+
+
+def deposit_kernel(me_ref, table_ref, slot_ref, out_ref, acc, sem):
     me = me_ref[0]
     zeros = jnp.zeros((8, 2048), F32)
 
@@ -235,15 +429,15 @@
             acc[q, FR : FR + 8, 2048 * j : 2048 * (j + 1)] = zeros
     lane = lax.broadcasted_iota(jnp.int32, (G + 8, 128), 1)
 
-    def place(index, slot):
-        row = row_ref[index]
+    def place(b, s, rank):
+        row = table_ref[b, 8 + s]
         r = pl.ds(pl.multiple_of(row // 8 * 8, 8), G + 8)
-        col = col_ref[index]
+        col = table_ref[b, 16 + s]
         tile = col // 128
         c = col % 128
         first = pl.ds(pl.multiple_of(tile * 128, 128), 128)
         second = pl.ds(pl.multiple_of(jnp.minimum(tile + 1, GY // 128 - 1) * 128, 128), 128)
-        patch = jnp.concatenate([slot_ref[slot], jnp.zeros((8, 2 * G), F32)], axis=0)
+        patch = jnp.concatenate([slot_ref[rank, b], jnp.zeros((8, 2 * G), F32)], axis=0)
         patch = pltpu.roll(patch, row % 8, 0)
         for q in range(2):
             part = jnp.where(lane < G, patch if q == 0 else pltpu.roll(patch, G, 1), 0.0)
@@ -251,22 +445,19 @@
             acc[q, r, first] += jnp.where(lane >= c, moved, 0.0)
             acc[q, r, second] += jnp.where(lane < c, moved, 0.0)
 
-    own = CAP
-
     def source(b, carry):
         seen = jnp.int32(0)
-        for s in range(own):
-            index = b * own + s
-            mine = owner_ref[index] == me
+        for s in range(8):
+            mine = table_ref[b, s] == me
 
             @pl.when(mine)
             def _():
-                place(index, seen * 16 + b)
+                place(b, s, seen)
 
             seen = seen + mine.astype(jnp.int32)
         return carry
 
-    lax.fori_loop(0, 16, source, 0)
+    lax.fori_loop(0, table_ref.shape[0], source, 0)
     copies = []
     for q in range(2):
         for j in range(8):
@@ -278,47 +469,27 @@
         copy.wait()
 
 
-def deposit(me, owners, rows, cols, slots):
+def deposit(me, table, slots):
     return pl.pallas_call(
         deposit_kernel,
         out_shape=jax.ShapeDtypeStruct((2, FR, GY), F32),
-        in_specs=[smem()] * 4 + [vmem()],
+        in_specs=[smem()] * 2 + [vmem()],
         out_specs=pl.BlockSpec(memory_space=pl.ANY),
         scratch_shapes=[pltpu.VMEM((2, FR + 8, GY), F32), pltpu.SemaphoreType.DMA((16,))],
         compiler_params=pltpu.CompilerParams(vmem_limit_bytes=48 << 20),
         name="deposit",
-    )(me, owners, rows, cols, slots)
-
-
-def slot_table(target, groups, depth):
-    total = target.shape[0]
-    hits = (target[:, None] == jnp.arange(groups, dtype=jnp.int32)[None, :]).astype(jnp.int32)
-    before = jnp.cumsum(hits, axis=0) - hits
-    ranking = jnp.sum(before * hits, axis=1)
-    placed = target * depth + ranking
-    match = placed[None, :] == jnp.arange(groups * depth, dtype=jnp.int32)[:, None]
-    source = jnp.sum(jnp.where(match, jnp.arange(total, dtype=jnp.int32)[None, :], 0), axis=1)
-    return source
+    )(me, table, slots)
 
 
 def per_device(visibilities, anchor, drift, target, subgrid_w, facet_owner, row_offset, col_offset):
-    base_count = lax.axis_size("base")
-    own = subgrid_w.shape[0]
-    first = (lax.axis_index("freq") * visibilities.shape[2]).astype(jnp.int32).reshape(1)
+    nb, nf = lax.axis_size("base"), lax.axis_size("freq")
     me = lax.axis_index("base").astype(jnp.int32).reshape(1)
+    owner = facet_owner[:, 0]
+    spot = jnp.concatenate([owner, row_offset, col_offset])
+    spot = jnp.pad(spot, (0, 128 - spot.shape[0])).reshape(1, 128)
     vr, vi, co = prep(target, visibilities, anchor, drift)
-    table = jnp.stack([facet_owner[:, 0], row_offset, col_offset])
-    table = lax.all_gather(table, "base", axis=1, tiled=True)
-    images = grid_all(first, vr, vi, co)
-    images = lax.psum_scatter(images, "base", scatter_dimension=0, tiled=True)
-    images = lax.psum(images, "freq")
-    consts = [jnp.asarray(x) for x in constants()]
-    patches = jax.vmap(lambda m, w: make_patch(m, w, *consts))(images, subgrid_w)
-    chosen = slot_table(facet_owner[:, 0], base_count, FCAP)
-    outgoing = jnp.take(patches, chosen, axis=0).reshape(base_count, FCAP, G, 2 * G)
-    arrived = lax.all_to_all(outgoing, "base", split_axis=0, concat_axis=0, tiled=True)
-    slots = jnp.moveaxis(arrived, 1, 0).reshape(FCAP * base_count, G, 2 * G)
-    return deposit(me, table[0], table[1], table[2], slots)
+    slots, table = main(owner, subgrid_w, spot, vr, vi, co, nb, nf)
+    return deposit(me, table, slots)
 
 
 def solution(mesh):

time: 280 us -> 114 us (0.41)
  the two profiles are of different devices: /device:TPU:22 before, /device:TPU:1 now
where the time goes in v2:
time: 114 us; the launch traced here: 112 us
  Pallas kernels  104 us (91%)
  local copies, waits for them, and re-layouts  7.95 us (7%)
    pallas_call x1, Pallas kernels, main(): pl.pallas_call(functools.partial(main_kernel, nb, nf), out_shape=(jax.Sha...  88.9 us
    pallas_call x1, Pallas kernels, deposit(): pl.pallas_call(deposit_kernel, out_shape=jax.ShapeDtypeStruct((2, FR, GY)...  10.2 us
    unnamed x20, local copies, waits for them, and re-layouts  7.95 us
    pallas_call x1, Pallas kernels, prep(): pl.pallas_call(prep_kernel, out_shape=(jax.ShapeDtypeStruct((blocks, chan...  4.6 us

profile of v2, /device:TPU:1, one launch (start us, length us, event | category | flops | bytes accessed | tf_op | source)
XLA Modules:
  0.0 112.4 jit_solution(12862751275865946198)
XLA Ops:
  0.0 0.8 pad_add_fusion
  0.8 0.0 copy-start
  0.8 1.2 %copy-done = bf16[2,1024,256]{2,1,0:T(8,128)(2,1)S(1)} copy-done((bf16[2,1024,256]{2,1,0:T(8,128)(2,1)S(1)}, bf16[2,1024,256]{2,1,0:T(8,128)(2,1)}, u32[]{:S(2)}) %copy-start) | copy-done | bytes 1048600
  2.0 0.0 copy-start.5
  2.0 0.7 copy-done.5
  2.7 0.0 copy-start.6
  2.7 0.7 copy-done.6
  3.4 0.0 copy-start.7
  3.4 0.7 copy-done.7
  4.1 4.6 %prep.1 = (f32[1024,256]{1,0:T(8,128)S(1)}, f32[1024,256]{1,0:T(8,128)S(1)}, f32[1024,4]{1,0:T(8,128)S(1)}) custom-call(s32[1,1024]{1,0:T(1,128)S(1)} %bitcast.5, bf16[2,1024,256]{2,1,0:T(8,128)(2,1)S(1)} %copy-done, bf16[2,1024]{1,0:T(2,128)(2,1)S(1)} %copy-done.6, bf16[2,1024]{1,0:T(2,128)(2,1)S(1)} %copy-done.7), custom_call_target="tpu_custom_call" | custom-call | tf_op jit(solution)/shard_map/prep/pallas_call | solution.py:61
  8.7 0.0 copy-start.1
  8.7 0.8 copy-done.1
  9.5 0.0 copy-start.2
  9.5 0.8 copy-done.2
  10.3 0.0 copy-start.3
  10.4 0.8 copy-done.3
  11.2 0.0 copy-start.4
  11.2 0.8 copy-done.4
  12.0 0.0 copy-start.8
  12.0 0.7 copy-done.8
  12.7 0.0 copy-start.9
  12.7 0.7 copy-done.9
  13.3 88.9 %main.1 = (f32[2,16,64,128]{3,2,1,0:T(8,128)S(1)}, s32[16,128]{1,0:T(8,128)S(1)}) custom-call(s32[8]{0:T(128)S(1)} %bitcast.7, f32[8]{0:T(128)S(1)} %copy-done.9, s32[1,128]{1,0:T(1,128)S(1)} %pad_bitcast_fusion.spot_ref, f32[1024,256]{1,0:T(8,128)S(1)} %get-tuple-element.10.vr_ref, f32[1024,256]{1,0:T(8,128)S(1)} %get-tuple-element.11.vi_ref, ...), custom_call_target="tpu_custom_call" | custom-call | tf_op jit(solution)/shard_map/main/pallas_call | solution.py:377
  102.2 10.2 %deposit.1 = f32[2,128,16384]{2,1,0:T(8,128)} custom-call(s32[1]{0:T(128)} %bitcast.me_ref, s32[16,128]{1,0:T(8,128)S(1)} %get-tuple-element.13.table_ref, f32[2,16,64,128]{3,2,1,0:T(8,128)S(1)} %get-tuple-element.14.slot_ref), custom_call_target="tpu_custom_call" | custom-call | tf_op jit(solution)/shard_map/deposit/pallas_call | solution.py:473
  (1 shorter events, 0.0 us)
Async XLA Ops:
  0.8 1.2 %copy-start = (bf16[2,1024,256]{2,1,0:T(8,128)(2,1)S(1)}, bf16[2,1024,256]{2,1,0:T(8,128)(2,1)}, u32[]{:S(2)}) copy-start(bf16[2,1024,256]{2,1,0:T(8,128)(2,1)} %vis_ref.1) | copy-start | bytes 3145732
  2.0 0.7 copy-start.5
  2.7 0.7 copy-start.6
  3.4 0.7 copy-start.7
  8.7 0.8 copy-start.1
  9.5 0.8 copy-start.2
  10.3 0.8 copy-start.3
  11.2 0.8 copy-start.4
  12.0 0.7 copy-start.8
  12.7 0.7 copy-start.9

commit v3 on v2

--- a/solution.py
+++ b/solution.py
@@ -25,11 +25,35 @@
     return pl.BlockSpec(memory_space=VMEM)
 
 
+def hbm():
+    return pl.BlockSpec(memory_space=pltpu.MemorySpace.HBM)
+
+
+def stay(x):
+    return pltpu.with_memory_space_constraint(x, pltpu.MemorySpace.HBM)
+
+
 def smem():
     return pl.BlockSpec(memory_space=SMEM)
 
 
-def prep_kernel(target_ref, vis_ref, anchor_ref, drift_ref, vr_ref, vi_ref, co_ref):
+CLEAR = 2048
+
+
+def prep_kernel(
+    target_hbm, vis_hbm, anchor_hbm, drift_hbm, vr_ref, vi_ref, co_ref, grid_ref, target_ref, vis_ref, anchor_ref, drift_ref, zeros, sem, zsem
+):
+    pairs = [(target_hbm, target_ref), (vis_hbm, vis_ref), (anchor_hbm, anchor_ref), (drift_hbm, drift_ref)]
+    loads = [pltpu.make_async_copy(src, dst, sem.at[i]) for i, (src, dst) in enumerate(pairs)]
+    for load in loads:
+        load.start()
+    zeros[...] = jnp.zeros(zeros.shape, F32)
+    clears = []
+    for q in range(2):
+        for j in range(GY // CLEAR):
+            part = grid_ref.at[q, :, CLEAR * j : CLEAR * (j + 1)]
+            clears.append(pltpu.make_async_copy(zeros, part, zsem.at[len(clears)]))
+    loads[0].wait()
     blocks = target_ref.shape[1]
     groups = blocks // CAP
     target = target_ref[...]
@@ -41,6 +65,10 @@
     ranking = jnp.sum(before * hits, axis=0, keepdims=True)
     placed = target * CAP + ranking.astype(jnp.int32)
     step = 128
+    for load in loads[1:]:
+        load.wait()
+    for clear in clears:
+        clear.start()
 
     def chunk(i, carry):
         start = pl.multiple_of(i * step, step)
@@ -54,6 +82,8 @@
         return carry
 
     lax.fori_loop(0, blocks // step, chunk, 0)
+    for clear in clears:
+        clear.wait()
 
 
 def prep(target, visibilities, anchor, drift):
@@ -64,12 +94,22 @@
             jax.ShapeDtypeStruct((blocks, channels), F32),
             jax.ShapeDtypeStruct((blocks, channels), F32),
             jax.ShapeDtypeStruct((blocks, 4), F32),
+            jax.ShapeDtypeStruct((2, FR, GY), F32),
         ),
-        in_specs=[vmem()] * 4,
-        out_specs=(vmem(), vmem(), vmem()),
+        in_specs=[hbm()] * 4,
+        out_specs=(vmem(), vmem(), vmem(), hbm()),
+        scratch_shapes=[
+            pltpu.VMEM((1, blocks), jnp.int32),
+            pltpu.VMEM(visibilities.shape, BF16),
+            pltpu.VMEM(anchor.shape, BF16),
+            pltpu.VMEM(drift.shape, BF16),
+            pltpu.VMEM((FR, CLEAR), F32),
+            pltpu.SemaphoreType.DMA((4,)),
+            pltpu.SemaphoreType.DMA((2 * GY // CLEAR,)),
+        ],
         compiler_params=pltpu.CompilerParams(vmem_limit_bytes=48 << 20),
         name="prep",
-    )(target.reshape(1, blocks), visibilities, anchor, drift)
+    )(target, visibilities, anchor, drift)
 
 
 def trig(h):
@@ -127,7 +167,7 @@
     return jnp.concatenate([a0, a1, a2, a3, b0, b1, b2, b3], axis=0)
 
 
-def one_subgrid(g, chan, vr_ref, vi_ref, co_ref, tx, ty, tv):
+def tables(g, chan, vr_ref, vi_ref, co_ref, tx, ty, tv):
     rows = pl.ds(pl.multiple_of(8 * g, 8), 8)
     co = co_ref[rows, :]
     hx = (co[:, 0:1] - 0.5 * G + chan * co[:, 2:3]) * (math.pi / G)
@@ -140,6 +180,9 @@
     vi = vi_ref[rows, :]
     tv[0:8, :] = vr * er + vi * ei
     tv[8:16, :] = vi * er - vr * ei
+
+
+def products(tx, ty, tv):
     acc = None
     for s in range(8):
         f = jnp.concatenate([expand(tx, s, h).astype(BF16) for h in (0, 1)], axis=1)
@@ -167,33 +210,58 @@
     right1 = np.block([[a.T, b.T], [-b.T, a.T]])
     left2 = np.concatenate([fr, fi], axis=0)
     right2 = np.block([[fr, fi], [-fi, fr]]) / G
-    return [x.astype(np.float32) for x in (left1, right1, left2, right2)]
+
+    def split(x):
+        high = x.astype(jnp.bfloat16)
+        return high, (x - high.astype(np.float64)).astype(jnp.bfloat16)
+
+    one_l, _ = split(left1)
+    one_r, _ = split(right1)
+    two_l, two_ll = split(left2)
+    two_r, two_rl = split(right2)
+    return [
+        np.concatenate([one_l, one_l], axis=1),
+        np.concatenate([one_r, one_r], axis=0),
+        np.concatenate([two_l, two_l, two_ll, 0 * two_l], axis=1),
+        np.concatenate([two_r, two_r, two_rl], axis=0),
+    ]
+
+
+def split_rows(x, times, axis):
+    high = x.astype(BF16)
+    low = (x - high.astype(F32)).astype(BF16)
+    return jnp.concatenate(([high, low] + [high] * 2)[:times], axis=axis)
+
+
+def dot16(a, b):
+    return jnp.dot(a, b, preferred_element_type=F32)
 
 
 def swap(x):
     return pltpu.roll(x, G, 1)
 
 
-def dot32(a, b):
-    return jnp.dot(a, b, precision=lax.Precision.HIGHEST, preferred_element_type=F32)
-
-
-def make_patch(m, w, left1, right1, left2, right2):
+def screen(w):
+    row = lax.broadcasted_iota(jnp.int32, (G, 2 * G), 0)
     lane = lax.broadcasted_iota(jnp.int32, (G, 2 * G), 1)
-    sign = jnp.where(lane < G, -1.0, 1.0).astype(F32)
-    row = lax.broadcasted_iota(jnp.int32, (G, 2 * G), 0)
     xl = (row - G // 2).astype(F32) * (2.0 / G)
-    xm = (lane % G - G // 2).astype(F32) * (2.0 / G)
+    xm = (jnp.where(lane < G, lane, lane - G) - G // 2).astype(F32) * (2.0 / G)
     c, s = trig((0.25 * math.pi) * w * (xl * xl + xm * xm))
     for _ in range(2):
         c, s = 2.0 * c * c - 1.0, 2.0 * c * s
-    both = dot32(left1, m)
+    return c, jnp.where(lane < G, -s, s)
+
+
+def make_patch(m, c, s, left1, right1, left2, right2):
+    lane = lax.broadcasted_iota(jnp.int32, (G, 2 * G), 1)
+    sign = jnp.where(lane < G, -1.0, 1.0).astype(F32)
+    both = dot16(left1, split_rows(m, 2, 0))
     y = both[:G] + sign * swap(both[G:])
-    z = dot32(y, right1)
-    k = z * c + swap(z) * (s * sign)
-    both = dot32(left2, k)
+    z = dot16(split_rows(y, 2, 1), right1)
+    k = z * c + swap(z) * s
+    both = dot16(left2, split_rows(k, 4, 0))
     y = both[:G] + sign * swap(both[G:])
-    return dot32(y, right2)
+    return dot16(split_rows(y, 3, 1), right2)
 
 
 MESH = pl.DeviceIdType.MESH
@@ -202,27 +270,42 @@
 def main_kernel(
     nb,
     nf,
-    owner_ref,
-    w_ref,
-    spot_ref,
+    owner_hbm,
+    row_hbm,
+    col_hbm,
+    w_hbm,
+    left1_hbm,
+    right1_hbm,
+    left2_hbm,
+    right2_hbm,
     vr_ref,
     vi_ref,
     co_ref,
+    slots,
+    table,
+    owner_ref,
+    row_ref,
+    col_ref,
+    w_ref,
     left1,
     right1,
     left2,
     right2,
-    slots,
-    table,
-    tx,
-    ty,
-    tv,
+    spot_ref,
+    tx0,
+    ty0,
+    tv0,
+    tx1,
+    ty1,
+    tv1,
+    cs,
     send,
     recv,
     total,
     fsum,
     gath,
     outb,
+    load_sem,
     spot_s,
     spot_r,
     base_s,
@@ -240,6 +323,8 @@
     me_f = lax.axis_index("freq")
     own = total.shape[0]
     core = me_f % 2
+    even = (tx0, ty0, tv0)
+    odd = (tx1, ty1, tv1)
 
     def base_copy(src, dst, ss, rs, t):
         return pltpu.make_async_remote_copy(
@@ -261,59 +346,91 @@
     barrier = pltpu.get_barrier_semaphore()
     each(1, nb, lambda t: pl.semaphore_signal(barrier, inc=1, device_id={"base": (me_b + t) % nb}, device_id_type=MESH))
     each(1, nf, lambda d: pl.semaphore_signal(barrier, inc=1, device_id={"freq": (me_f + d) % nf}, device_id_type=MESH))
-    pl.semaphore_wait(barrier, nb + nf - 2)
+    pairs = [
+        (owner_hbm, owner_ref),
+        (row_hbm, row_ref),
+        (col_hbm, col_ref),
+        (w_hbm, w_ref),
+        (left1_hbm, left1),
+        (right1_hbm, right1),
+        (left2_hbm, left2),
+        (right2_hbm, right2),
+    ]
+    loads = [pltpu.make_async_copy(src, dst, load_sem.at[i]) for i, (src, dst) in enumerate(pairs)]
+    for load in loads:
+        load.start()
+
+    channels = vr_ref.shape[1]
+    chan = (lax.broadcasted_iota(jnp.int32, (8, channels), 1) + me_f * channels).astype(F32)
+
+    def subgrid(i):
+        return (me_b + 1 + i // own) % nb * own + i % own
+
+    def prepare(i, tabs):
+        tables(subgrid(i), chan, vr_ref, vi_ref, co_ref, *tabs)
 
     def spot_copy(t):
         return base_copy(spot_ref, table.at[pl.ds(me_b, 1)], spot_s.at[t - 1], spot_r.at[t - 1], t)
 
-    each(1, nb, lambda t: spot_copy(t).start())
-    table[pl.ds(me_b, 1), :] = spot_ref[...]
-
-    channels = vr_ref.shape[1]
-    chan = (lax.broadcasted_iota(jnp.int32, (8, channels), 1) + me_f * channels).astype(F32)
-
     def share_copy(t):
         return base_copy(send.at[t], recv.at[t], base_s.at[t], base_r.at[t], t + 1)
 
+    prepare(0, even)
+    for load in loads:
+        load.wait()
+    lane = lax.broadcasted_iota(jnp.int32, (1, 128), 1)
+    spot = jnp.zeros((1, 128), jnp.int32)
+    for n, ref in enumerate((owner_ref, row_ref, col_ref)):
+        for i in range(own):
+            spot = jnp.where(lane == n * own + i, ref[0, i], spot)
+    spot_ref[...] = spot
+    table[pl.ds(me_b, 1), :] = spot
+    c, s = screen(w_ref[0, me_f])
+    cs[0] = c
+    cs[1] = s
+
     def group(t):
-        owner = (me_b + 1 + t) % nb
-
-        def one(j):
-            g = owner * own + j
-            send[t, j] = one_subgrid(g, chan, vr_ref, vi_ref, co_ref, tx, ty, tv).astype(BF16)
-
-        each(0, own, one)
+        def two(u):
+            i = t * own + 2 * u
+            prepare(i + 1, odd)
+            send[t, 2 * u] = products(*even).astype(BF16)
+            prepare(i + 2, even)
+            send[t, 2 * u + 1] = products(*odd).astype(BF16)
+
+        each(0, own // 2, two)
+
+        @pl.when(t == 0)
+        def _():
+            pl.semaphore_wait(barrier, nb + nf - 2)
+            each(1, nb, lambda t: spot_copy(t).start())
 
         @pl.when(t < nb - 1)
         def _():
             share_copy(t).start()
 
     each(0, nb, group)
-
-    def own_share(j):
-        total[j] = send[nb - 1, j].astype(F32)
-
-    each(0, own, own_share)
-
-    def add_share(t):
-        share_copy(t).wait_recv()
-
-        def add(j):
-            total[j] += recv[t, j].astype(F32)
-
-        each(0, own, add)
-
-    each(0, nb - 1, add_share)
+    each(0, nb - 1, lambda t: share_copy(t).wait_recv())
+
+    def sum_shares(j):
+        m = send[nb - 1, j].astype(F32)
+        for t in range(nb - 1):
+            m = m + recv[t, j].astype(F32)
+        return m
 
     def sum_copy(d):
         return freq_copy(total.at[(me_f + d) % nf], fsum.at[d - 1], freq_s.at[d - 1], freq_r.at[d - 1], d)
 
-    each(1, nf, lambda d: sum_copy(d).start())
-    m = total[me_f]
+    def reduce(d):
+        j = (me_f + d) % nf
+        total[j] = sum_shares(j)
+        sum_copy(d).start()
+
+    each(1, nf, reduce)
+    m = sum_shares(me_f)
+    each(1, nf, lambda d: sum_copy(d).wait_recv())
     for d in range(1, nf):
-        sum_copy(d).wait_recv()
         m = m + fsum[d - 1]
-    gath[me_f] = make_patch(m, w_ref[me_f], left1[...], right1[...], left2[...], right2[...])
+    gath[me_f] = make_patch(m, cs[0], cs[1], left1[...], right1[...], left2[...], right2[...])
 
     def gath_copy(d):
         return freq_copy(gath.at[me_f], gath.at[me_f], gath_s.at[d - 1], gath_r.at[d - 1], d)
@@ -328,7 +445,7 @@
         seen = jnp.int32(0)
         index = jnp.int32(0)
         for s in range(own):
-            hit = (owner_ref[s] == o).astype(jnp.int32)
+            hit = (owner_ref[0, s] == o).astype(jnp.int32)
             use = hit * (seen == core).astype(jnp.int32)
             index = index + use * s
             seen = seen + hit
@@ -369,29 +486,38 @@
     each(1, nb, lambda t: spot_copy(t).wait())
 
 
-def main(owner, w, spot, vr, vi, co, nb, nf):
-    own = w.shape[0]
+def main(owner, row, col, w, vr, vi, co, nb, nf):
+    own = w.shape[1]
     unit = (G, 2 * G)
     dma = pltpu.SemaphoreType.DMA
-    consts = [jnp.asarray(x) for x in constants()]
+    consts = [stay(jnp.asarray(x)) for x in constants()]
+    tabs = [pltpu.VMEM((2 * HALF, 128), F32), pltpu.VMEM((2 * HALF, 128), F32), pltpu.VMEM((16, 256), F32)]
     return pl.pallas_call(
         functools.partial(main_kernel, nb, nf),
         out_shape=(
             jax.ShapeDtypeStruct((FCAP, nb) + unit, F32),
             jax.ShapeDtypeStruct((nb, 128), jnp.int32),
         ),
-        in_specs=[smem()] * 2 + [vmem()] * 8,
+        in_specs=[hbm()] * 8 + [vmem()] * 3,
         out_specs=(vmem(), vmem()),
         scratch_shapes=[
-            pltpu.VMEM((2 * HALF, 128), F32),
-            pltpu.VMEM((2 * HALF, 128), F32),
-            pltpu.VMEM((16, 256), F32),
+            pltpu.SMEM((1, own), jnp.int32),
+            pltpu.SMEM((1, own), jnp.int32),
+            pltpu.SMEM((1, own), jnp.int32),
+            pltpu.SMEM((1, own), F32),
+        ]
+        + [pltpu.VMEM(x.shape, BF16) for x in consts]
+        + [pltpu.VMEM((1, 128), jnp.int32)]
+        + tabs * 2
+        + [
+            pltpu.VMEM((2,) + unit, F32),
             pltpu.VMEM((nb, own) + unit, BF16),
             pltpu.VMEM((nb - 1, own) + unit, BF16),
             pltpu.VMEM((own,) + unit, F32),
             pltpu.VMEM((nf - 1,) + unit, F32),
             pltpu.VMEM((nf,) + unit, F32),
             pltpu.VMEM((nb,) + unit, F32),
+            dma((8,)),
             dma((nb - 1,)),
             dma((nb - 1,)),
             dma((nb - 1,)),
@@ -409,25 +535,32 @@
             vmem_limit_bytes=48 << 20, collective_id=0, has_side_effects=True
         ),
         name="main",
-    )(owner, w, spot, vr, vi, co, *consts)
-
-
-def deposit_kernel(me_ref, table_ref, slot_ref, out_ref, acc, sem):
-    me = me_ref[0]
-    zeros = jnp.zeros((8, 2048), F32)
-
-    def clear(i, carry):
-        q = i // (FR // 8)
-        r = pl.ds(pl.multiple_of((i % (FR // 8)) * 8, 8), 8)
-        for j in range(GY // 2048):
-            acc[q, r, 2048 * j : 2048 * (j + 1)] = zeros
+    )(owner, row, col, w, *consts, vr, vi, co)
+
+
+def deposit_kernel(table_ref, slot_ref, grid_in, grid_ref, blocks, where_ref, tile_ref, count_ref, sem):
+    del grid_in
+    me = lax.axis_index("base")
+    tiles = GY // 128
+
+    def reset(i, carry):
+        where_ref[i] = -1
         return carry
 
-    lax.fori_loop(0, 2 * FR // 8, clear, 0)
-    for q in range(2):
-        for j in range(GY // 2048):
-            acc[q, FR : FR + 8, 2048 * j : 2048 * (j + 1)] = zeros
+    lax.fori_loop(0, tiles, reset, 0)
+    count_ref[0] = 0
     lane = lax.broadcasted_iota(jnp.int32, (G + 8, 128), 1)
+
+    def block_of(tile):
+        @pl.when(where_ref[tile] < 0)
+        def _():
+            count = count_ref[0]
+            where_ref[tile] = count
+            tile_ref[count] = tile
+            count_ref[0] = count + 1
+            blocks[count] = jnp.zeros(blocks.shape[1:], F32)
+
+        return where_ref[tile]
 
     def place(b, s, rank):
         row = table_ref[b, 8 + s]
@@ -435,15 +568,19 @@
         col = table_ref[b, 16 + s]
         tile = col // 128
         c = col % 128
-        first = pl.ds(pl.multiple_of(tile * 128, 128), 128)
-        second = pl.ds(pl.multiple_of(jnp.minimum(tile + 1, GY // 128 - 1) * 128, 128), 128)
         patch = jnp.concatenate([slot_ref[rank, b], jnp.zeros((8, 2 * G), F32)], axis=0)
         patch = pltpu.roll(patch, row % 8, 0)
-        for q in range(2):
-            part = jnp.where(lane < G, patch if q == 0 else pltpu.roll(patch, G, 1), 0.0)
-            moved = pltpu.roll(part, c, 1)
-            acc[q, r, first] += jnp.where(lane >= c, moved, 0.0)
-            acc[q, r, second] += jnp.where(lane < c, moved, 0.0)
+        real = pltpu.roll(jnp.where(lane < G, patch, 0.0), c, 1)
+        imag = pltpu.roll(jnp.where(lane < G, 0.0, patch), c + G, 1)
+        first = block_of(tile)
+        blocks[first, 0, r, :] += jnp.where(lane >= c, real, 0.0)
+        blocks[first, 1, r, :] += jnp.where(lane >= c, imag, 0.0)
+
+        @pl.when(c > 128 - G)
+        def _():
+            second = block_of(tile + 1)
+            blocks[second, 0, r, :] += jnp.where(lane < c, real, 0.0)
+            blocks[second, 1, r, :] += jnp.where(lane < c, imag, 0.0)
 
     def source(b, carry):
         seen = jnp.int32(0)
@@ -458,38 +595,51 @@
         return carry
 
     lax.fori_loop(0, table_ref.shape[0], source, 0)
-    copies = []
-    for q in range(2):
-        for j in range(8):
-            r = pl.ds(j * 16, 16)
-            copies.append(pltpu.make_async_copy(acc.at[q, r], out_ref.at[q, r], sem.at[q * 8 + j]))
-    for copy in copies:
-        copy.start()
-    for copy in copies:
-        copy.wait()
-
-
-def deposit(me, table, slots):
+    count = count_ref[0]
+
+    def copy(i):
+        cut = pl.ds(pl.multiple_of(tile_ref[i] * 128, 128), 128)
+        return pltpu.make_async_copy(blocks.at[i, :, 0:FR, :], grid_ref.at[:, :, cut], sem.at[i])
+
+    def start(i, carry):
+        copy(i).start()
+        return carry
+
+    def wait(i, carry):
+        copy(i).wait()
+        return carry
+
+    lax.fori_loop(0, count, start, 0)
+    lax.fori_loop(0, count, wait, 0)
+
+
+def deposit(table, slots, grid):
+    most = 2 * slots.shape[0] * slots.shape[1]
     return pl.pallas_call(
         deposit_kernel,
         out_shape=jax.ShapeDtypeStruct((2, FR, GY), F32),
-        in_specs=[smem()] * 2 + [vmem()],
-        out_specs=pl.BlockSpec(memory_space=pl.ANY),
-        scratch_shapes=[pltpu.VMEM((2, FR + 8, GY), F32), pltpu.SemaphoreType.DMA((16,))],
+        in_specs=[smem(), vmem(), hbm()],
+        out_specs=hbm(),
+        scratch_shapes=[
+            pltpu.VMEM((most, 2, FR + 8, 128), F32),
+            pltpu.SMEM((GY // 128,), jnp.int32),
+            pltpu.SMEM((most,), jnp.int32),
+            pltpu.SMEM((1,), jnp.int32),
+            pltpu.SemaphoreType.DMA((most,)),
+        ],
+        input_output_aliases={2: 0},
         compiler_params=pltpu.CompilerParams(vmem_limit_bytes=48 << 20),
         name="deposit",
-    )(me, table, slots)
+    )(table, slots, grid)
 
 
 def per_device(visibilities, anchor, drift, target, subgrid_w, facet_owner, row_offset, col_offset):
     nb, nf = lax.axis_size("base"), lax.axis_size("freq")
-    me = lax.axis_index("base").astype(jnp.int32).reshape(1)
-    owner = facet_owner[:, 0]
-    spot = jnp.concatenate([owner, row_offset, col_offset])
-    spot = jnp.pad(spot, (0, 128 - spot.shape[0])).reshape(1, 128)
-    vr, vi, co = prep(target, visibilities, anchor, drift)
-    slots, table = main(owner, subgrid_w, spot, vr, vi, co, nb, nf)
-    return deposit(me, table, slots)
+    target = target.reshape(1, -1)
+    vr, vi, co, grid = prep(*[stay(x) for x in (target, visibilities, anchor, drift)])
+    small = [stay(x.reshape(1, -1)) for x in (facet_owner, row_offset, col_offset, subgrid_w)]
+    slots, table = main(*small, vr, vi, co, nb, nf)
+    return deposit(table, slots, grid)
 
 
 def solution(mesh):

time: 114 us -> 88.3 us (0.77)
  the two profiles are of different devices: /device:TPU:1 before, /device:TPU:41 now
where the time goes in v3:
time: 88.3 us; the launch traced here: 88.1 us
  Pallas kernels  88.1 us (100%)
    pallas_call x1, Pallas kernels, main(): pl.pallas_call(functools.partial(main_kernel, nb, nf), out_shape=(jax.Sha...  71.4 us
    pallas_call x1, Pallas kernels, deposit(): pl.pallas_call(deposit_kernel, out_shape=jax.ShapeDtypeStruct((2, FR, GY)...  9.47 us
    pallas_call x1, Pallas kernels, prep(): pl.pallas_call(prep_kernel, out_shape=(jax.ShapeDtypeStruct((blocks, chan...  7.24 us

profile of v3, /device:TPU:41, one launch (start us, length us, event | category | flops | bytes accessed | tf_op | source)
XLA Modules:
  0.0 88.1 jit_solution(3421762773321850081)
XLA Ops:
  0.0 7.2 %prep.1 = (f32[1024,256]{1,0:T(8,128)S(1)}, f32[1024,256]{1,0:T(8,128)S(1)}, f32[1024,4]{1,0:T(8,128)S(1)}, f32[2,128,16384]{2,1,0:T(8,128)}) custom-call(s32[1,1024]{1,0:T(1,128)} %bitcast.5, bf16[2,1024,256]{2,1,0:T(8,128)(2,1)} %vis_hbm.1, bf16[2,1024]{1,0:T(2,128)(2,1)} %anchor_hbm.1, bf16[2,1024]{1,0:T(2,128)(2,1)} %drift_hbm.1), custom_call_target="tpu_custom_call" | custom-call | tf_op jit(solution)/shard_map/prep/pallas_call | solution.py:91
  7.2 71.4 %main.1 = (f32[2,16,64,128]{3,2,1,0:T(8,128)S(1)}, s32[16,128]{1,0:T(8,128)S(1)}) custom-call(s32[1,8]{1,0:T(1,128)} %bitcast.6, s32[1,8]{1,0:T(1,128)} %bitcast.7, s32[1,8]{1,0:T(1,128)} %bitcast.8, f32[1,8]{1,0:T(1,128)} %bitcast.9, bf16[128,128]{1,0:T(8,128)(2,1)} %constant.8.clone.left1_hbm, bf16[256,128]{1,0:T(8,128)(2,1)} %constant.9.clone.right1_hbm, ...), custom_call_target="tpu_custom_call" | custom-call | tf_op jit(solution)/shard_map/main/pallas_call | solution.py:495
  78.7 9.5 %deposit.1 = f32[2,128,16384]{2,1,0:T(8,128)} custom-call(s32[16,128]{1,0:T(8,128)S(1)} %get-tuple-element.14.table_ref, f32[2,16,64,128]{3,2,1,0:T(8,128)S(1)} %get-tuple-element.15.slot_ref, f32[2,128,16384]{2,1,0:T(8,128)} %get-tuple-element.16.grid_in), custom_call_target="tpu_custom_call", output_to_operand_aliasing={{}: (2, {})} | custom-call | tf_op jit(solution)/shard_map/deposit/pallas_call | solution.py:618

commit v4 on v3

--- a/solution.py
+++ b/solution.py
@@ -53,6 +53,8 @@
         for j in range(GY // CLEAR):
             part = grid_ref.at[q, :, CLEAR * j : CLEAR * (j + 1)]
             clears.append(pltpu.make_async_copy(zeros, part, zsem.at[len(clears)]))
+    for clear in clears:
+        clear.start()
     loads[0].wait()
     blocks = target_ref.shape[1]
     groups = blocks // CAP
@@ -67,8 +69,6 @@
     step = 128
     for load in loads[1:]:
         load.wait()
-    for clear in clears:
-        clear.start()
 
     def chunk(i, carry):
         start = pl.multiple_of(i * step, step)
@@ -265,6 +265,7 @@
 
 
 MESH = pl.DeviceIdType.MESH
+CHUNKS = 2
 
 
 def main_kernel(
@@ -299,13 +300,19 @@
     ty1,
     tv1,
     cs,
+    part,
+    got,
     send,
     recv,
     total,
     fsum,
-    gath,
+    gath0,
+    gath1,
     outb,
+    choice,
     load_sem,
+    core_s,
+    core_r,
     spot_s,
     spot_r,
     base_s,
@@ -321,8 +328,10 @@
 ):
     me_b = lax.axis_index("base")
     me_f = lax.axis_index("freq")
-    own = total.shape[0]
+    own = w_ref.shape[1]
     core = me_f % 2
+    place = me_f // 2
+    half = own // 2
     even = (tx0, ty0, tv0)
     odd = (tx1, ty1, tv1)
 
@@ -372,6 +381,9 @@
     def spot_copy(t):
         return base_copy(spot_ref, table.at[pl.ds(me_b, 1)], spot_s.at[t - 1], spot_r.at[t - 1], t)
 
+    def core_copy(t):
+        return freq_copy(part.at[t, 1 - core], got.at[t], core_s.at[t], core_r.at[t], 1 - 2 * core + nf)
+
     def share_copy(t):
         return base_copy(send.at[t], recv.at[t], base_s.at[t], base_r.at[t], t + 1)
 
@@ -389,100 +401,124 @@
     cs[0] = c
     cs[1] = s
 
+    def choose(o):
+        seen = jnp.int32(0)
+        index = jnp.int32(0)
+        for s in range(own):
+            hit = (owner_ref[0, s] == o).astype(jnp.int32)
+            index = index + hit * (seen == core).astype(jnp.int32) * s
+            seen = seen + hit
+        choice[o] = index
+
+    each(0, nb, choose)
+
+    def send_share(t):
+        core_copy(t).wait_recv()
+        for i in range(half):
+            send[t, i] = (part[t, core, i] + got[t, i]).astype(BF16)
+        share_copy(t).start()
+
     def group(t):
         def two(u):
             i = t * own + 2 * u
             prepare(i + 1, odd)
-            send[t, 2 * u] = products(*even).astype(BF16)
+            part[t, 0, u] = products(*even)
             prepare(i + 2, even)
-            send[t, 2 * u + 1] = products(*odd).astype(BF16)
-
-        each(0, own // 2, two)
+            part[t, 1, u] = products(*odd)
+
+        each(0, 1, two)
 
         @pl.when(t == 0)
         def _():
             pl.semaphore_wait(barrier, nb + nf - 2)
             each(1, nb, lambda t: spot_copy(t).start())
 
-        @pl.when(t < nb - 1)
+        @pl.when(t > 0)
         def _():
-            share_copy(t).start()
+            send_share(t - 1)
+
+        each(1, half, two)
+
+        core_copy(t).start()
 
     each(0, nb, group)
     each(0, nb - 1, lambda t: share_copy(t).wait_recv())
-
-    def sum_shares(j):
-        m = send[nb - 1, j].astype(F32)
+    core_copy(nb - 1).wait_recv()
+
+    def sum_shares(i):
+        m = part[nb - 1, core, i] + got[nb - 1, i]
         for t in range(nb - 1):
-            m = m + recv[t, j].astype(F32)
+            m = m + recv[t, i].astype(F32)
         return m
 
+    chips = nf // 2
+
     def sum_copy(d):
-        return freq_copy(total.at[(me_f + d) % nf], fsum.at[d - 1], freq_s.at[d - 1], freq_r.at[d - 1], d)
+        return freq_copy(total.at[(place + d) % chips], fsum.at[d - 1], freq_s.at[d - 1], freq_r.at[d - 1], 2 * d)
 
     def reduce(d):
-        j = (me_f + d) % nf
-        total[j] = sum_shares(j)
+        i = (place + d) % chips
+        total[i] = sum_shares(i)
         sum_copy(d).start()
 
-    each(1, nf, reduce)
-    m = sum_shares(me_f)
-    each(1, nf, lambda d: sum_copy(d).wait_recv())
-    for d in range(1, nf):
+    each(1, chips, reduce)
+    m = sum_shares(place)
+    each(1, chips, lambda d: sum_copy(d).wait_recv())
+    for d in range(1, chips):
         m = m + fsum[d - 1]
-    gath[me_f] = make_patch(m, cs[0], cs[1], left1[...], right1[...], left2[...], right2[...])
-
-    def gath_copy(d):
-        return freq_copy(gath.at[me_f], gath.at[me_f], gath_s.at[d - 1], gath_r.at[d - 1], d)
-
-    each(1, nf, lambda d: gath_copy(d).start())
-    each(1, nf, lambda d: gath_copy(d).wait_recv())
-
-    def out_copy(t):
-        return base_copy(outb.at[(me_b + t) % nb], slots.at[core, me_b], out_s.at[t - 1], out_r.at[t - 1], t)
-
-    def pick(o):
-        seen = jnp.int32(0)
-        index = jnp.int32(0)
-        for s in range(own):
-            hit = (owner_ref[0, s] == o).astype(jnp.int32)
-            use = hit * (seen == core).astype(jnp.int32)
-            index = index + use * s
-            seen = seen + hit
-        return gath[index]
-
-    def ship(t):
-        o = (me_b + t) % nb
-        outb[o] = pick(o)
-        out_copy(t).start()
-
-    each(1, nb, ship)
-    slots[core, me_b] = pick(me_b)
-
-    def pair_copy(t):
-        source = (me_b + nb - t) % nb
-        part = slots.at[core, source]
-        return pltpu.make_async_remote_copy(
-            src_ref=part,
-            dst_ref=part,
-            send_sem=pair_s.at[t],
-            recv_sem=pair_r.at[t],
-            device_id={"freq": me_f + 1 - 2 * core},
-            device_id_type=MESH,
+    patch = make_patch(m, cs[0], cs[1], left1[...], right1[...], left2[...], right2[...])
+    gath = (gath0, gath1)
+    for chunk in range(CHUNKS):
+        gath[chunk][me_f] = patch[chunk * (G // CHUNKS) : (chunk + 1) * (G // CHUNKS)]
+
+    def rows_of(chunk):
+        return pl.ds(chunk * (G // CHUNKS), G // CHUNKS)
+
+    def gath_copy(chunk, d):
+        piece = gath[chunk].at[me_f]
+        return freq_copy(piece, piece, gath_s.at[chunk, d - 1], gath_r.at[chunk, d - 1], d)
+
+    def out_copy(chunk, t):
+        return base_copy(
+            outb.at[(me_b + t) % nb, rows_of(chunk)],
+            slots.at[core, me_b, rows_of(chunk)],
+            out_s.at[chunk, t - 1],
+            out_r.at[chunk, t - 1],
+            t,
         )
 
-    pair_copy(0).start()
-
-    def forward(t):
-        out_copy(t).wait_recv()
-        pair_copy(t).start()
-
-    each(1, nb, forward)
-    each(0, nb, lambda t: pair_copy(t).wait())
-    each(1, nb, lambda t: out_copy(t).wait_send())
-    each(1, nf, lambda d: gath_copy(d).wait_send())
-    each(1, nf, lambda d: sum_copy(d).wait_send())
+    def pair_copy(chunk, t):
+        piece = slots.at[core, (me_b + nb - t) % nb, rows_of(chunk)]
+        return freq_copy(piece, piece, pair_s.at[chunk, t], pair_r.at[chunk, t], 1 - 2 * core + nf)
+
+    for chunk in range(CHUNKS):
+        each(1, nf, lambda d: gath_copy(chunk, d).start())
+    for chunk in range(CHUNKS):
+        each(1, nf, lambda d: gath_copy(chunk, d).wait_recv())
+        rows = rows_of(chunk)
+
+        def ship(t):
+            o = (me_b + t) % nb
+            outb[o, rows] = gath[chunk][choice[o]]
+            out_copy(chunk, t).start()
+
+        each(1, nb, ship)
+        slots[core, me_b, rows] = gath[chunk][choice[me_b]]
+        pair_copy(chunk, 0).start()
+    for chunk in range(CHUNKS):
+
+        def forward(t):
+            out_copy(chunk, t).wait_recv()
+            pair_copy(chunk, t).start()
+
+        each(1, nb, forward)
+    for chunk in range(CHUNKS):
+        each(0, nb, lambda t: pair_copy(chunk, t).wait())
+        each(1, nb, lambda t: out_copy(chunk, t).wait_send())
+        each(1, nf, lambda d: gath_copy(chunk, d).wait_send())
+    each(1, chips, lambda d: sum_copy(d).wait_send())
     each(0, nb - 1, lambda t: share_copy(t).wait_send())
+    each(0, nb, lambda t: core_copy(t).wait_send())
     each(1, nb, lambda t: spot_copy(t).wait())
 
 
@@ -511,25 +547,31 @@
         + tabs * 2
         + [
             pltpu.VMEM((2,) + unit, F32),
-            pltpu.VMEM((nb, own) + unit, BF16),
-            pltpu.VMEM((nb - 1, own) + unit, BF16),
-            pltpu.VMEM((own,) + unit, F32),
-            pltpu.VMEM((nf - 1,) + unit, F32),
-            pltpu.VMEM((nf,) + unit, F32),
+            pltpu.VMEM((nb, 2, own // 2) + unit, F32),
+            pltpu.VMEM((nb, own // 2) + unit, F32),
+            pltpu.VMEM((nb - 1, own // 2) + unit, BF16),
+            pltpu.VMEM((nb - 1, own // 2) + unit, BF16),
+            pltpu.VMEM((own // 2,) + unit, F32),
+            pltpu.VMEM((nf // 2 - 1,) + unit, F32),
+            pltpu.VMEM((nf, G // CHUNKS, 2 * G), F32),
+            pltpu.VMEM((nf, G // CHUNKS, 2 * G), F32),
             pltpu.VMEM((nb,) + unit, F32),
+            pltpu.SMEM((nb,), jnp.int32),
             dma((8,)),
+            dma((nb,)),
+            dma((nb,)),
             dma((nb - 1,)),
             dma((nb - 1,)),
             dma((nb - 1,)),
             dma((nb - 1,)),
-            dma((nf - 1,)),
-            dma((nf - 1,)),
-            dma((nf - 1,)),
-            dma((nf - 1,)),
-            dma((nb - 1,)),
-            dma((nb - 1,)),
-            dma((nb,)),
-            dma((nb,)),
+            dma((nf // 2 - 1,)),
+            dma((nf // 2 - 1,)),
+            dma((CHUNKS, nf - 1)),
+            dma((CHUNKS, nf - 1)),
+            dma((CHUNKS, nb - 1)),
+            dma((CHUNKS, nb - 1)),
+            dma((CHUNKS, nb)),
+            dma((CHUNKS, nb)),
         ],
         compiler_params=pltpu.CompilerParams(
             vmem_limit_bytes=48 << 20, collective_id=0, has_side_effects=True

time: 88.3 us -> 90.6 us (1.026)
  the two profiles are of different devices: /device:TPU:41 before, /device:TPU:1 now
where the time goes in v4:
time: 90.6 us; the launch traced here: 90.4 us
  Pallas kernels  90.4 us (100%)
    pallas_call x1, Pallas kernels, main(): pl.pallas_call(functools.partial(main_kernel, nb, nf), out_shape=(jax.Sha...  78.7 us
    pallas_call x1, Pallas kernels, prep(): pl.pallas_call(prep_kernel, out_shape=(jax.ShapeDtypeStruct((blocks, chan...  6.46 us
    pallas_call x1, Pallas kernels, deposit(): pl.pallas_call(deposit_kernel, out_shape=jax.ShapeDtypeStruct((2, FR, GY)...  5.26 us

profile of v4, /device:TPU:1, one launch (start us, length us, event | category | flops | bytes accessed | tf_op | source)
XLA Modules:
  0.0 90.4 jit_solution(10469167567523527090)
XLA Ops:
  0.0 6.5 %prep.1 = (f32[1024,256]{1,0:T(8,128)S(1)}, f32[1024,256]{1,0:T(8,128)S(1)}, f32[1024,4]{1,0:T(8,128)S(1)}, f32[2,128,16384]{2,1,0:T(8,128)}) custom-call(s32[1,1024]{1,0:T(1,128)} %bitcast.5, bf16[2,1024,256]{2,1,0:T(8,128)(2,1)} %vis_hbm.1, bf16[2,1024]{1,0:T(2,128)(2,1)} %anchor_hbm.1, bf16[2,1024]{1,0:T(2,128)(2,1)} %drift_hbm.1), custom_call_target="tpu_custom_call" | custom-call | tf_op jit(solution)/shard_map/prep/pallas_call | solution.py:91
  6.5 78.7 %main.1 = (f32[2,16,64,128]{3,2,1,0:T(8,128)S(1)}, s32[16,128]{1,0:T(8,128)S(1)}) custom-call(s32[1,8]{1,0:T(1,128)} %bitcast.6, s32[1,8]{1,0:T(1,128)} %bitcast.7, s32[1,8]{1,0:T(1,128)} %bitcast.8, f32[1,8]{1,0:T(1,128)} %bitcast.9, bf16[128,128]{1,0:T(8,128)(2,1)} %constant.8.clone.left1_hbm, bf16[256,128]{1,0:T(8,128)(2,1)} %constant.9.clone.right1_hbm, ...), custom_call_target="tpu_custom_call" | custom-call | tf_op jit(solution)/shard_map/main/pallas_call | solution.py:531
  85.1 5.3 %deposit.1 = f32[2,128,16384]{2,1,0:T(8,128)} custom-call(s32[16,128]{1,0:T(8,128)S(1)} %get-tuple-element.14.table_ref, f32[2,16,64,128]{3,2,1,0:T(8,128)S(1)} %get-tuple-element.15.slot_ref, f32[2,128,16384]{2,1,0:T(8,128)} %get-tuple-element.16.grid_in), custom_call_target="tpu_custom_call", output_to_operand_aliasing={{}: (2, {})} | custom-call | tf_op jit(solution)/shard_map/deposit/pallas_call | solution.py:660

commit v5 on v3

--- a/solution.py
+++ b/solution.py
@@ -53,6 +53,8 @@
         for j in range(GY // CLEAR):
             part = grid_ref.at[q, :, CLEAR * j : CLEAR * (j + 1)]
             clears.append(pltpu.make_async_copy(zeros, part, zsem.at[len(clears)]))
+    for clear in clears:
+        clear.start()
     loads[0].wait()
     blocks = target_ref.shape[1]
     groups = blocks // CAP
@@ -67,8 +69,6 @@
     step = 128
     for load in loads[1:]:
         load.wait()
-    for clear in clears:
-        clear.start()
 
     def chunk(i, carry):
         start = pl.multiple_of(i * step, step)
@@ -305,6 +305,7 @@
     fsum,
     gath,
     outb,
+    choice,
     load_sem,
     spot_s,
     spot_r,
@@ -326,9 +327,16 @@
     even = (tx0, ty0, tv0)
     odd = (tx1, ty1, tv1)
 
+    side = math.isqrt(nb)
+
+    def peer(t, sign):
+        z = (me_b // side + side + sign * (t % side)) % side
+        y = (me_b % side + side + sign * ((t // side + t) % side)) % side
+        return z * side + y
+
     def base_copy(src, dst, ss, rs, t):
         return pltpu.make_async_remote_copy(
-            src_ref=src, dst_ref=dst, send_sem=ss, recv_sem=rs, device_id={"base": (me_b + t) % nb}, device_id_type=MESH
+            src_ref=src, dst_ref=dst, send_sem=ss, recv_sem=rs, device_id={"base": peer(t, 1)}, device_id_type=MESH
         )
 
     def freq_copy(src, dst, ss, rs, d):
@@ -364,7 +372,7 @@
     chan = (lax.broadcasted_iota(jnp.int32, (8, channels), 1) + me_f * channels).astype(F32)
 
     def subgrid(i):
-        return (me_b + 1 + i // own) % nb * own + i % own
+        return peer(i // own + 1, 1) * own + i % own
 
     def prepare(i, tabs):
         tables(subgrid(i), chan, vr_ref, vi_ref, co_ref, *tabs)
@@ -389,6 +397,17 @@
     cs[0] = c
     cs[1] = s
 
+    def choose(o):
+        seen = jnp.int32(0)
+        index = jnp.int32(0)
+        for s in range(own):
+            hit = (owner_ref[0, s] == o).astype(jnp.int32)
+            index = index + hit * (seen == core).astype(jnp.int32) * s
+            seen = seen + hit
+        choice[o] = index
+
+    each(0, nb, choose)
+
     def group(t):
         def two(u):
             i = t * own + 2 * u
@@ -439,20 +458,13 @@
     each(1, nf, lambda d: gath_copy(d).wait_recv())
 
     def out_copy(t):
-        return base_copy(outb.at[(me_b + t) % nb], slots.at[core, me_b], out_s.at[t - 1], out_r.at[t - 1], t)
+        return base_copy(outb.at[peer(t, 1)], slots.at[core, me_b], out_s.at[t - 1], out_r.at[t - 1], t)
 
     def pick(o):
-        seen = jnp.int32(0)
-        index = jnp.int32(0)
-        for s in range(own):
-            hit = (owner_ref[0, s] == o).astype(jnp.int32)
-            use = hit * (seen == core).astype(jnp.int32)
-            index = index + use * s
-            seen = seen + hit
-        return gath[index]
+        return gath[choice[o]]
 
     def ship(t):
-        o = (me_b + t) % nb
+        o = peer(t, 1)
         outb[o] = pick(o)
         out_copy(t).start()
 
@@ -460,7 +472,7 @@
     slots[core, me_b] = pick(me_b)
 
     def pair_copy(t):
-        source = (me_b + nb - t) % nb
+        source = peer(t, -1)
         part = slots.at[core, source]
         return pltpu.make_async_remote_copy(
             src_ref=part,
@@ -517,6 +529,7 @@
             pltpu.VMEM((nf - 1,) + unit, F32),
             pltpu.VMEM((nf,) + unit, F32),
             pltpu.VMEM((nb,) + unit, F32),
+            pltpu.SMEM((nb,), jnp.int32),
             dma((8,)),
             dma((nb - 1,)),
             dma((nb - 1,)),

time: 88.3 us -> 89.1 us (level)
  the two profiles are of different devices: /device:TPU:41 before, /device:TPU:9 now
where the time goes in v5:
time: 89.1 us; the launch traced here: 89 us
  Pallas kernels  88.9 us (100%)
    pallas_call x1, Pallas kernels, main(): pl.pallas_call(functools.partial(main_kernel, nb, nf), out_shape=(jax.Sha...  73 us
    pallas_call x1, Pallas kernels, deposit(): pl.pallas_call(deposit_kernel, out_shape=jax.ShapeDtypeStruct((2, FR, GY)...  9.51 us
    pallas_call x1, Pallas kernels, prep(): pl.pallas_call(prep_kernel, out_shape=(jax.ShapeDtypeStruct((blocks, chan...  6.46 us

profile of v5, /device:TPU:9, one launch (start us, length us, event | category | flops | bytes accessed | tf_op | source)
XLA Modules:
  0.0 89.0 jit_solution(9508983373877782959)
XLA Ops:
  0.0 6.5 %prep.1 = (f32[1024,256]{1,0:T(8,128)S(1)}, f32[1024,256]{1,0:T(8,128)S(1)}, f32[1024,4]{1,0:T(8,128)S(1)}, f32[2,128,16384]{2,1,0:T(8,128)}) custom-call(s32[1,1024]{1,0:T(1,128)} %bitcast.5, bf16[2,1024,256]{2,1,0:T(8,128)(2,1)} %vis_hbm.1, bf16[2,1024]{1,0:T(2,128)(2,1)} %anchor_hbm.1, bf16[2,1024]{1,0:T(2,128)(2,1)} %drift_hbm.1), custom_call_target="tpu_custom_call" | custom-call | tf_op jit(solution)/shard_map/prep/pallas_call | solution.py:91
  6.5 73.0 %main.1 = (f32[2,16,64,128]{3,2,1,0:T(8,128)S(1)}, s32[16,128]{1,0:T(8,128)S(1)}) custom-call(s32[1,8]{1,0:T(1,128)} %bitcast.6, s32[1,8]{1,0:T(1,128)} %bitcast.7, s32[1,8]{1,0:T(1,128)} %bitcast.8, f32[1,8]{1,0:T(1,128)} %bitcast.9, bf16[128,128]{1,0:T(8,128)(2,1)} %constant.8.clone.left1_hbm, bf16[256,128]{1,0:T(8,128)(2,1)} %constant.9.clone.right1_hbm, ...), custom_call_target="tpu_custom_call" | custom-call | tf_op jit(solution)/shard_map/main/pallas_call | solution.py:507
  79.5 9.5 %deposit.1 = f32[2,128,16384]{2,1,0:T(8,128)} custom-call(s32[16,128]{1,0:T(8,128)S(1)} %get-tuple-element.14.table_ref, f32[2,16,64,128]{3,2,1,0:T(8,128)S(1)} %get-tuple-element.15.slot_ref, f32[2,128,16384]{2,1,0:T(8,128)} %get-tuple-element.16.grid_in), custom_call_target="tpu_custom_call", output_to_operand_aliasing={{}: (2, {})} | custom-call | tf_op jit(solution)/shard_map/deposit/pallas_call | solution.py:631

commit v6 on v5

--- a/solution.py
+++ b/solution.py
@@ -38,6 +38,14 @@
 
 
 CLEAR = 2048
+PIECES = 2 * GY // CLEAR
+EARLY = PIECES - 4
+
+
+def clear_copy(zeros, grid_ref, sem, i, first):
+    j = i % (GY // CLEAR)
+    part = grid_ref.at[i // (GY // CLEAR), :, CLEAR * j : CLEAR * (j + 1)]
+    return pltpu.make_async_copy(zeros, part, sem.at[i - first])
 
 
 def prep_kernel(
@@ -48,11 +56,7 @@
     for load in loads:
         load.start()
     zeros[...] = jnp.zeros(zeros.shape, F32)
-    clears = []
-    for q in range(2):
-        for j in range(GY // CLEAR):
-            part = grid_ref.at[q, :, CLEAR * j : CLEAR * (j + 1)]
-            clears.append(pltpu.make_async_copy(zeros, part, zsem.at[len(clears)]))
+    clears = [clear_copy(zeros, grid_ref, zsem, i, 0) for i in range(EARLY)]
     for clear in clears:
         clear.start()
     loads[0].wait()
@@ -105,7 +109,7 @@
             pltpu.VMEM(drift.shape, BF16),
             pltpu.VMEM((FR, CLEAR), F32),
             pltpu.SemaphoreType.DMA((4,)),
-            pltpu.SemaphoreType.DMA((2 * GY // CLEAR,)),
+            pltpu.SemaphoreType.DMA((EARLY,)),
         ],
         compiler_params=pltpu.CompilerParams(vmem_limit_bytes=48 << 20),
         name="prep",
@@ -378,35 +382,37 @@
         tables(subgrid(i), chan, vr_ref, vi_ref, co_ref, *tabs)
 
     def spot_copy(t):
-        return base_copy(spot_ref, table.at[pl.ds(me_b, 1)], spot_s.at[t - 1], spot_r.at[t - 1], t)
+        return base_copy(spot_ref.at[pl.ds(peer(t, 1), 1)], table.at[pl.ds(me_b, 1)], spot_s.at[t - 1], spot_r.at[t - 1], t)
 
     def share_copy(t):
         return base_copy(send.at[t], recv.at[t], base_s.at[t], base_r.at[t], t + 1)
 
     prepare(0, even)
-    for load in loads:
-        load.wait()
     lane = lax.broadcasted_iota(jnp.int32, (1, 128), 1)
-    spot = jnp.zeros((1, 128), jnp.int32)
-    for n, ref in enumerate((owner_ref, row_ref, col_ref)):
-        for i in range(own):
-            spot = jnp.where(lane == n * own + i, ref[0, i], spot)
-    spot_ref[...] = spot
-    table[pl.ds(me_b, 1), :] = spot
-    c, s = screen(w_ref[0, me_f])
-    cs[0] = c
-    cs[1] = s
 
     def choose(o):
         seen = jnp.int32(0)
-        index = jnp.int32(0)
+        index = [jnp.int32(0)] * FCAP
         for s in range(own):
             hit = (owner_ref[0, s] == o).astype(jnp.int32)
-            index = index + hit * (seen == core).astype(jnp.int32) * s
+            index = [index[r] + hit * (seen == r).astype(jnp.int32) * s for r in range(FCAP)]
             seen = seen + hit
-        choice[o] = index
-
-    each(0, nb, choose)
+        choice[o] = index[0] * (1 - core) + index[1] * core
+        spot = jnp.zeros((1, 128), jnp.int32)
+        for r in range(FCAP):
+            fields = ((seen > r).astype(jnp.int32), row_ref[0, index[r]], col_ref[0, index[r]])
+            for n, value in enumerate(fields):
+                spot = jnp.where(lane == 3 * r + n, value, spot)
+        spot_ref[pl.ds(o, 1), :] = spot
+
+    def small_work():
+        for load in loads:
+            load.wait()
+        c, s = screen(w_ref[0, me_f])
+        cs[0] = c
+        cs[1] = s
+        each(0, nb, choose)
+        table[pl.ds(me_b, 1), :] = spot_ref[pl.ds(me_b, 1), :]
 
     def group(t):
         def two(u):
@@ -421,11 +427,15 @@
         @pl.when(t == 0)
         def _():
             pl.semaphore_wait(barrier, nb + nf - 2)
-            each(1, nb, lambda t: spot_copy(t).start())
 
         @pl.when(t < nb - 1)
         def _():
             share_copy(t).start()
+
+        @pl.when(t == 0)
+        def _():
+            small_work()
+            each(1, nb, lambda t: spot_copy(t).start())
 
     each(0, nb, group)
     each(0, nb - 1, lambda t: share_copy(t).wait_recv())
@@ -519,7 +529,7 @@
             pltpu.SMEM((1, own), F32),
         ]
         + [pltpu.VMEM(x.shape, BF16) for x in consts]
-        + [pltpu.VMEM((1, 128), jnp.int32)]
+        + [pltpu.VMEM((nb, 128), jnp.int32)]
         + tabs * 2
         + [
             pltpu.VMEM((2,) + unit, F32),
@@ -551,9 +561,12 @@
     )(owner, row, col, w, *consts, vr, vi, co)
 
 
-def deposit_kernel(table_ref, slot_ref, grid_in, grid_ref, blocks, where_ref, tile_ref, count_ref, sem):
+def deposit_kernel(table_ref, slot_ref, grid_in, grid_ref, zeros, blocks, where_ref, tile_ref, count_ref, sem, zsem):
     del grid_in
-    me = lax.axis_index("base")
+    zeros[...] = jnp.zeros(zeros.shape, F32)
+    clears = [clear_copy(zeros, grid_ref, zsem, i, EARLY) for i in range(EARLY, PIECES)]
+    for clear in clears:
+        clear.start()
     tiles = GY // 128
 
     def reset(i, carry):
@@ -575,10 +588,10 @@
 
         return where_ref[tile]
 
-    def place(b, s, rank):
-        row = table_ref[b, 8 + s]
+    def place(b, rank):
+        row = table_ref[b, 3 * rank + 1]
         r = pl.ds(pl.multiple_of(row // 8 * 8, 8), G + 8)
-        col = table_ref[b, 16 + s]
+        col = table_ref[b, 3 * rank + 2]
         tile = col // 128
         c = col % 128
         patch = jnp.concatenate([slot_ref[rank, b], jnp.zeros((8, 2 * G), F32)], axis=0)
@@ -596,15 +609,12 @@
             blocks[second, 1, r, :] += jnp.where(lane < c, imag, 0.0)
 
     def source(b, carry):
-        seen = jnp.int32(0)
-        for s in range(8):
-            mine = table_ref[b, s] == me
-
-            @pl.when(mine)
+        for rank in range(FCAP):
+
+            @pl.when(table_ref[b, 3 * rank] > 0)
             def _():
-                place(b, s, seen)
-
-            seen = seen + mine.astype(jnp.int32)
+                place(b, rank)
+
         return carry
 
     lax.fori_loop(0, table_ref.shape[0], source, 0)
@@ -622,6 +632,8 @@
         copy(i).wait()
         return carry
 
+    for clear in clears:
+        clear.wait()
     lax.fori_loop(0, count, start, 0)
     lax.fori_loop(0, count, wait, 0)
 
@@ -634,11 +646,13 @@
         in_specs=[smem(), vmem(), hbm()],
         out_specs=hbm(),
         scratch_shapes=[
+            pltpu.VMEM((FR, CLEAR), F32),
             pltpu.VMEM((most, 2, FR + 8, 128), F32),
             pltpu.SMEM((GY // 128,), jnp.int32),
             pltpu.SMEM((most,), jnp.int32),
             pltpu.SMEM((1,), jnp.int32),
             pltpu.SemaphoreType.DMA((most,)),
+            pltpu.SemaphoreType.DMA((PIECES - EARLY,)),
         ],
         input_output_aliases={2: 0},
         compiler_params=pltpu.CompilerParams(vmem_limit_bytes=48 << 20),

time: 89.1 us -> 87 us (0.976)
  the two profiles are of different devices: /device:TPU:9 before, /device:TPU:33 now
where the time goes in v6:
time: 87 us; the launch traced here: 86.9 us
  Pallas kernels  86.9 us (100%)
    pallas_call x1, Pallas kernels, main(): pl.pallas_call(functools.partial(main_kernel, nb, nf), out_shape=(jax.Sha...  71.6 us
    pallas_call x1, Pallas kernels, deposit(): pl.pallas_call(deposit_kernel, out_shape=jax.ShapeDtypeStruct((2, FR, GY)...  8.86 us
    pallas_call x1, Pallas kernels, prep(): pl.pallas_call(prep_kernel, out_shape=(jax.ShapeDtypeStruct((blocks, chan...  6.41 us

profile of v6, /device:TPU:33, one launch (start us, length us, event | category | flops | bytes accessed | tf_op | source)
XLA Modules:
  0.0 86.9 jit_solution(16738642881631643587)
XLA Ops:
  0.0 6.4 %prep.1 = (f32[1024,256]{1,0:T(8,128)S(1)}, f32[1024,256]{1,0:T(8,128)S(1)}, f32[1024,4]{1,0:T(8,128)S(1)}, f32[2,128,16384]{2,1,0:T(8,128)}) custom-call(s32[1,1024]{1,0:T(1,128)} %bitcast.5, bf16[2,1024,256]{2,1,0:T(8,128)(2,1)} %vis_hbm.1, bf16[2,1024]{1,0:T(2,128)(2,1)} %anchor_hbm.1, bf16[2,1024]{1,0:T(2,128)(2,1)} %drift_hbm.1), custom_call_target="tpu_custom_call" | custom-call | tf_op jit(solution)/shard_map/prep/pallas_call | solution.py:95
  6.4 71.6 %main.1 = (f32[2,16,64,128]{3,2,1,0:T(8,128)S(1)}, s32[16,128]{1,0:T(8,128)S(1)}) custom-call(s32[1,8]{1,0:T(1,128)} %bitcast.6, s32[1,8]{1,0:T(1,128)} %bitcast.7, s32[1,8]{1,0:T(1,128)} %bitcast.8, f32[1,8]{1,0:T(1,128)} %bitcast.9, bf16[128,128]{1,0:T(8,128)(2,1)} %constant.8.clone.left1_hbm, bf16[256,128]{1,0:T(8,128)(2,1)} %constant.9.clone.right1_hbm, ...), custom_call_target="tpu_custom_call" | custom-call | tf_op jit(solution)/shard_map/main/pallas_call | solution.py:517
  78.0 8.9 %deposit.1 = f32[2,128,16384]{2,1,0:T(8,128)} custom-call(s32[16,128]{1,0:T(8,128)S(1)} %get-tuple-element.14.table_ref, f32[2,16,64,128]{3,2,1,0:T(8,128)S(1)} %get-tuple-element.15.slot_ref, f32[2,128,16384]{2,1,0:T(8,128)} %get-tuple-element.16.grid_in), custom_call_target="tpu_custom_call", output_to_operand_aliasing={{}: (2, {})} | custom-call | tf_op jit(solution)/shard_map/deposit/pallas_call | solution.py:643

commit v7 on v6

--- a/solution.py
+++ b/solution.py
@@ -49,7 +49,7 @@
 
 
 def prep_kernel(
-    target_hbm, vis_hbm, anchor_hbm, drift_hbm, vr_ref, vi_ref, co_ref, grid_ref, target_ref, vis_ref, anchor_ref, drift_ref, zeros, sem, zsem
+    target_hbm, vis_hbm, anchor_hbm, drift_hbm, vr_ref, vi_ref, co_ref, grid_ref, target_ref, vis_ref, anchor_ref, drift_ref, pick_ref, zeros, sem, zsem
 ):
     pairs = [(target_hbm, target_ref), (vis_hbm, vis_ref), (anchor_hbm, anchor_ref), (drift_hbm, drift_ref)]
     loads = [pltpu.make_async_copy(src, dst, sem.at[i]) for i, (src, dst) in enumerate(pairs)]
@@ -62,30 +62,41 @@
     loads[0].wait()
     blocks = target_ref.shape[1]
     groups = blocks // CAP
-    target = target_ref[...]
-    hits = (lax.broadcasted_iota(jnp.int32, (groups, blocks), 0) == target).astype(F32)
-    earlier = lax.broadcasted_iota(jnp.int32, (blocks, blocks), 0) < lax.broadcasted_iota(
-        jnp.int32, (blocks, blocks), 1
+    width = 128
+    rows = lax.broadcasted_iota(jnp.int32, (width, width), 0)
+    lanes = lax.broadcasted_iota(jnp.int32, (width, width), 1)
+    count = jnp.concatenate([(rows < lanes).astype(F32), jnp.ones((width, width), F32)], axis=1)
+    ids = lax.broadcasted_iota(jnp.int32, (groups, width), 0)
+    pieces = range(blocks // width)
+    targets = [target_ref[:, width * i : width * (i + 1)] for i in pieces]
+    hits = [(ids == target).astype(F32) for target in targets]
+    counts = jnp.dot(
+        jnp.concatenate(hits, axis=0).astype(BF16), count.astype(BF16), preferred_element_type=F32
     )
-    before = jnp.dot(hits.astype(BF16), earlier.astype(F32).astype(BF16), preferred_element_type=F32)
-    ranking = jnp.sum(before * hits, axis=0, keepdims=True)
-    placed = target * CAP + ranking.astype(jnp.int32)
+    seen = jnp.zeros((groups, width), F32)
+    placed = []
+    for i in pieces:
+        inside = counts[groups * i : groups * (i + 1)]
+        ranking = jnp.sum((inside[:, :width] + seen) * hits[i], axis=0, keepdims=True)
+        placed.append(targets[i] * CAP + ranking.astype(jnp.int32))
+        seen = seen + inside[:, width:]
+    placed = jnp.concatenate(placed, axis=1)
     step = 128
+
+    def choose(i, carry):
+        start = pl.multiple_of(i * step, step)
+        match = lax.broadcasted_iota(jnp.int32, (step, blocks), 0) + start == placed
+        pick_ref[pl.ds(start, step), :] = match.astype(F32).astype(BF16)
+        return carry
+
+    lax.fori_loop(0, blocks // step, choose, 0)
     for load in loads[1:]:
         load.wait()
-
-    def chunk(i, carry):
-        start = pl.multiple_of(i * step, step)
-        rows = pl.ds(start, step)
-        match = lax.broadcasted_iota(jnp.int32, (step, blocks), 0) + start == placed
-        pick = match.astype(F32).astype(BF16)
-        vr_ref[rows, :] = jnp.dot(pick, vis_ref[0], preferred_element_type=F32)
-        vi_ref[rows, :] = jnp.dot(pick, vis_ref[1], preferred_element_type=F32)
-        co_ref[rows, 0:2] = lax.dot_general(pick, anchor_ref[...], NT, preferred_element_type=F32)
-        co_ref[rows, 2:4] = lax.dot_general(pick, drift_ref[...], NT, preferred_element_type=F32)
-        return carry
-
-    lax.fori_loop(0, blocks // step, chunk, 0)
+    pick = pick_ref[...]
+    places = jnp.concatenate([anchor_ref[...].astype(F32), drift_ref[...].astype(F32)], axis=0).astype(BF16)
+    co_ref[...] = lax.dot_general(pick, places, NT, preferred_element_type=F32)
+    vr_ref[...] = jnp.dot(pick, vis_ref[0], preferred_element_type=F32)
+    vi_ref[...] = jnp.dot(pick, vis_ref[1], preferred_element_type=F32)
     for clear in clears:
         clear.wait()
 
@@ -107,6 +118,7 @@
             pltpu.VMEM(visibilities.shape, BF16),
             pltpu.VMEM(anchor.shape, BF16),
             pltpu.VMEM(drift.shape, BF16),
+            pltpu.VMEM((blocks, blocks), BF16),
             pltpu.VMEM((FR, CLEAR), F32),
             pltpu.SemaphoreType.DMA((4,)),
             pltpu.SemaphoreType.DMA((EARLY,)),

time: 87 us -> 85.8 us (0.986)
  Pallas kernels: 86.9 us -> 85.6 us
    pallas_call x1, Pallas kernels: 6.41 us -> 4.76 us  [prep(): pl.pallas_call(prep_kernel, out_shape=(jax.ShapeDtypeStruct((blocks, chan...]
where the time goes in v7:
time: 85.8 us; the launch traced here: 85.6 us
  Pallas kernels  85.6 us (100%)
    pallas_call x1, Pallas kernels, main(): pl.pallas_call(functools.partial(main_kernel, nb, nf), out_shape=(jax.Sha...  71.6 us
    pallas_call x1, Pallas kernels, deposit(): pl.pallas_call(deposit_kernel, out_shape=jax.ShapeDtypeStruct((2, FR, GY)...  9.25 us
    pallas_call x1, Pallas kernels, prep(): pl.pallas_call(prep_kernel, out_shape=(jax.ShapeDtypeStruct((blocks, chan...  4.76 us

profile of v7, /device:TPU:33, one launch (start us, length us, event | category | flops | bytes accessed | tf_op | source)
XLA Modules:
  0.0 85.6 jit_solution(6743494750945227439)
XLA Ops:
  0.0 4.8 %prep.1 = (f32[1024,256]{1,0:T(8,128)S(1)}, f32[1024,256]{1,0:T(8,128)S(1)}, f32[1024,4]{1,0:T(8,128)S(1)}, f32[2,128,16384]{2,1,0:T(8,128)}) custom-call(s32[1,1024]{1,0:T(1,128)} %bitcast.5, bf16[2,1024,256]{2,1,0:T(8,128)(2,1)} %vis_hbm.1, bf16[2,1024]{1,0:T(2,128)(2,1)} %anchor_hbm.1, bf16[2,1024]{1,0:T(2,128)(2,1)} %drift_hbm.1), custom_call_target="tpu_custom_call" | custom-call | tf_op jit(solution)/shard_map/prep/pallas_call | solution.py:106
  4.8 71.6 %main.1 = (f32[2,16,64,128]{3,2,1,0:T(8,128)S(1)}, s32[16,128]{1,0:T(8,128)S(1)}) custom-call(s32[1,8]{1,0:T(1,128)} %bitcast.6, s32[1,8]{1,0:T(1,128)} %bitcast.7, s32[1,8]{1,0:T(1,128)} %bitcast.8, f32[1,8]{1,0:T(1,128)} %bitcast.9, bf16[128,128]{1,0:T(8,128)(2,1)} %constant.8.clone.left1_hbm, bf16[256,128]{1,0:T(8,128)(2,1)} %constant.9.clone.right1_hbm, ...), custom_call_target="tpu_custom_call" | custom-call | tf_op jit(solution)/shard_map/main/pallas_call | solution.py:529
  76.4 9.2 %deposit.1 = f32[2,128,16384]{2,1,0:T(8,128)} custom-call(s32[16,128]{1,0:T(8,128)S(1)} %get-tuple-element.14.table_ref, f32[2,16,64,128]{3,2,1,0:T(8,128)S(1)} %get-tuple-element.15.slot_ref, f32[2,128,16384]{2,1,0:T(8,128)} %get-tuple-element.16.grid_in), custom_call_target="tpu_custom_call", output_to_operand_aliasing={{}: (2, {})} | custom-call | tf_op jit(solution)/shard_map/deposit/pallas_call | solution.py:655

commit v8 on v7

--- a/solution.py
+++ b/solution.py
@@ -39,7 +39,7 @@
 
 CLEAR = 2048
 PIECES = 2 * GY // CLEAR
-EARLY = PIECES - 4
+EARLY = PIECES - 5
 
 
 def clear_copy(zeros, grid_ref, sem, i, first):
@@ -331,6 +331,8 @@
     freq_r,
     gath_s,
     gath_r,
+    hand_s,
+    hand_r,
     out_s,
     out_r,
     pair_s,
@@ -473,11 +475,24 @@
         m = m + fsum[d - 1]
     gath[me_f] = make_patch(m, cs[0], cs[1], left1[...], right1[...], left2[...], right2[...])
 
+    chips = nf // 2
+    turn = 1 - 2 * core + nf
+
     def gath_copy(d):
-        return freq_copy(gath.at[me_f], gath.at[me_f], gath_s.at[d - 1], gath_r.at[d - 1], d)
-
-    each(1, nf, lambda d: gath_copy(d).start())
-    each(1, nf, lambda d: gath_copy(d).wait_recv())
+        return freq_copy(gath.at[me_f], gath.at[me_f], gath_s.at[d - 1], gath_r.at[d - 1], 2 * d)
+
+    def hand_copy(d):
+        piece = gath.at[(me_f + nf - 2 * d) % nf]
+        return freq_copy(piece, piece, hand_s.at[d], hand_r.at[d], turn)
+
+    def hand_on(d):
+        gath_copy(d).wait_recv()
+        hand_copy(d).start()
+
+    each(1, chips, lambda d: gath_copy(d).start())
+    hand_copy(0).start()
+    each(1, chips, hand_on)
+    each(0, chips, lambda d: hand_copy(d).wait_recv())
 
     def out_copy(t):
         return base_copy(outb.at[peer(t, 1)], slots.at[core, me_b], out_s.at[t - 1], out_r.at[t - 1], t)
@@ -514,7 +529,8 @@
     each(1, nb, forward)
     each(0, nb, lambda t: pair_copy(t).wait())
     each(1, nb, lambda t: out_copy(t).wait_send())
-    each(1, nf, lambda d: gath_copy(d).wait_send())
+    each(1, chips, lambda d: gath_copy(d).wait_send())
+    each(0, chips, lambda d: hand_copy(d).wait_send())
     each(1, nf, lambda d: sum_copy(d).wait_send())
     each(0, nb - 1, lambda t: share_copy(t).wait_send())
     each(1, nb, lambda t: spot_copy(t).wait())
@@ -559,8 +575,10 @@
             dma((nb - 1,)),
             dma((nf - 1,)),
             dma((nf - 1,)),
-            dma((nf - 1,)),
-            dma((nf - 1,)),
+            dma((nf // 2 - 1,)),
+            dma((nf // 2 - 1,)),
+            dma((nf // 2,)),
+            dma((nf // 2,)),
             dma((nb - 1,)),
             dma((nb - 1,)),
             dma((nb,)),

time: 85.8 us -> 86.9 us (1.013)
  the two profiles are of different devices: /device:TPU:33 before, /device:TPU:1 now
where the time goes in v8:
time: 86.9 us; the launch traced here: 86.7 us
  Pallas kernels  86.7 us (100%)
    pallas_call x1, Pallas kernels, main(): pl.pallas_call(functools.partial(main_kernel, nb, nf), out_shape=(jax.Sha...  73.4 us
    pallas_call x1, Pallas kernels, deposit(): pl.pallas_call(deposit_kernel, out_shape=jax.ShapeDtypeStruct((2, FR, GY)...  8.89 us
    pallas_call x1, Pallas kernels, prep(): pl.pallas_call(prep_kernel, out_shape=(jax.ShapeDtypeStruct((blocks, chan...  4.44 us

profile of v8, /device:TPU:1, one launch (start us, length us, event | category | flops | bytes accessed | tf_op | source)
XLA Modules:
  0.0 86.7 jit_solution(199886373051639195)
XLA Ops:
  0.0 4.4 %prep.1 = (f32[1024,256]{1,0:T(8,128)S(1)}, f32[1024,256]{1,0:T(8,128)S(1)}, f32[1024,4]{1,0:T(8,128)S(1)}, f32[2,128,16384]{2,1,0:T(8,128)}) custom-call(s32[1,1024]{1,0:T(1,128)} %bitcast.5, bf16[2,1024,256]{2,1,0:T(8,128)(2,1)} %vis_hbm.1, bf16[2,1024]{1,0:T(2,128)(2,1)} %anchor_hbm.1, bf16[2,1024]{1,0:T(2,128)(2,1)} %drift_hbm.1), custom_call_target="tpu_custom_call" | custom-call | tf_op jit(solution)/shard_map/prep/pallas_call | solution.py:106
  4.4 73.4 %main.1 = (f32[2,16,64,128]{3,2,1,0:T(8,128)S(1)}, s32[16,128]{1,0:T(8,128)S(1)}) custom-call(s32[1,8]{1,0:T(1,128)} %bitcast.6, s32[1,8]{1,0:T(1,128)} %bitcast.7, s32[1,8]{1,0:T(1,128)} %bitcast.8, f32[1,8]{1,0:T(1,128)} %bitcast.9, bf16[128,128]{1,0:T(8,128)(2,1)} %constant.8.clone.left1_hbm, bf16[256,128]{1,0:T(8,128)(2,1)} %constant.9.clone.right1_hbm, ...), custom_call_target="tpu_custom_call" | custom-call | tf_op jit(solution)/shard_map/main/pallas_call | solution.py:545
  77.8 8.9 %deposit.1 = f32[2,128,16384]{2,1,0:T(8,128)} custom-call(s32[16,128]{1,0:T(8,128)S(1)} %get-tuple-element.14.table_ref, f32[2,16,64,128]{3,2,1,0:T(8,128)S(1)} %get-tuple-element.15.slot_ref, f32[2,128,16384]{2,1,0:T(8,128)} %get-tuple-element.16.grid_in), custom_call_target="tpu_custom_call", output_to_operand_aliasing={{}: (2, {})} | custom-call | tf_op jit(solution)/shard_map/deposit/pallas_call | solution.py:673

commit v9 on v8

--- a/solution.py
+++ b/solution.py
@@ -318,6 +318,7 @@
     send,
     recv,
     total,
+    csum,
     fsum,
     gath,
     outb,
@@ -327,6 +328,8 @@
     spot_r,
     base_s,
     base_r,
+    core_s,
+    core_r,
     freq_s,
     freq_r,
     gath_s,
@@ -340,8 +343,9 @@
 ):
     me_b = lax.axis_index("base")
     me_f = lax.axis_index("freq")
-    own = total.shape[0]
+    own = nf
     core = me_f % 2
+    place = me_f // 2
     even = (tx0, ty0, tv0)
     odd = (tx1, ty1, tv1)
 
@@ -460,23 +464,37 @@
             m = m + recv[t, j].astype(F32)
         return m
 
+    chips = nf // 2
+    turn = 1 - 2 * core + nf
+
+    def core_copy(i):
+        return freq_copy(total.at[1 - core, i], csum.at[i], core_s.at[i], core_r.at[i], turn)
+
     def sum_copy(d):
-        return freq_copy(total.at[(me_f + d) % nf], fsum.at[d - 1], freq_s.at[d - 1], freq_r.at[d - 1], d)
+        return freq_copy(total.at[core, (place + d) % chips], fsum.at[d - 1], freq_s.at[d - 1], freq_r.at[d - 1], 2 * d)
+
+    def offer(d):
+        i = (place + d) % chips
+        total[1 - core, i] = sum_shares(2 * i + 1 - core)
+        core_copy(i).start()
+
+    def join(i):
+        m = sum_shares(2 * i + core)
+        core_copy(i).wait_recv()
+        return m + csum[i]
 
     def reduce(d):
-        j = (me_f + d) % nf
-        total[j] = sum_shares(j)
+        i = (place + d) % chips
+        total[core, i] = join(i)
         sum_copy(d).start()
 
-    each(1, nf, reduce)
-    m = sum_shares(me_f)
-    each(1, nf, lambda d: sum_copy(d).wait_recv())
-    for d in range(1, nf):
+    each(1, chips + 1, offer)
+    each(1, chips, reduce)
+    m = join(place)
+    each(1, chips, lambda d: sum_copy(d).wait_recv())
+    for d in range(1, chips):
         m = m + fsum[d - 1]
     gath[me_f] = make_patch(m, cs[0], cs[1], left1[...], right1[...], left2[...], right2[...])
-
-    chips = nf // 2
-    turn = 1 - 2 * core + nf
 
     def gath_copy(d):
         return freq_copy(gath.at[me_f], gath.at[me_f], gath_s.at[d - 1], gath_r.at[d - 1], 2 * d)
@@ -531,7 +549,8 @@
     each(1, nb, lambda t: out_copy(t).wait_send())
     each(1, chips, lambda d: gath_copy(d).wait_send())
     each(0, chips, lambda d: hand_copy(d).wait_send())
-    each(1, nf, lambda d: sum_copy(d).wait_send())
+    each(1, chips, lambda d: sum_copy(d).wait_send())
+    each(0, chips, lambda i: core_copy(i).wait_send())
     each(0, nb - 1, lambda t: share_copy(t).wait_send())
     each(1, nb, lambda t: spot_copy(t).wait())
 
@@ -563,8 +582,9 @@
             pltpu.VMEM((2,) + unit, F32),
             pltpu.VMEM((nb, own) + unit, BF16),
             pltpu.VMEM((nb - 1, own) + unit, BF16),
-            pltpu.VMEM((own,) + unit, F32),
-            pltpu.VMEM((nf - 1,) + unit, F32),
+            pltpu.VMEM((2, nf // 2) + unit, F32),
+            pltpu.VMEM((nf // 2,) + unit, F32),
+            pltpu.VMEM((nf // 2 - 1,) + unit, F32),
             pltpu.VMEM((nf,) + unit, F32),
             pltpu.VMEM((nb,) + unit, F32),
             pltpu.SMEM((nb,), jnp.int32),
@@ -573,8 +593,10 @@
             dma((nb - 1,)),
             dma((nb - 1,)),
             dma((nb - 1,)),
-            dma((nf - 1,)),
-            dma((nf - 1,)),
+            dma((nf // 2,)),
+            dma((nf // 2,)),
+            dma((nf // 2 - 1,)),
+            dma((nf // 2 - 1,)),
             dma((nf // 2 - 1,)),
             dma((nf // 2 - 1,)),
             dma((nf // 2,)),

time: 86.9 us -> 82.7 us (0.952)
  Pallas kernels: 86.7 us -> 82.4 us
    pallas_call x1, Pallas kernels: 8.89 us -> 4.87 us  [deposit(): pl.pallas_call(deposit_kernel, out_shape=jax.ShapeDtypeStruct((2, FR, GY)...]
where the time goes in v9:
time: 82.7 us; the launch traced here: 82.5 us
  Pallas kernels  82.4 us (100%)
    pallas_call x1, Pallas kernels, main(): pl.pallas_call(functools.partial(main_kernel, nb, nf), out_shape=(jax.Sha...  73.1 us
    pallas_call x1, Pallas kernels, deposit(): pl.pallas_call(deposit_kernel, out_shape=jax.ShapeDtypeStruct((2, FR, GY)...  4.87 us
    pallas_call x1, Pallas kernels, prep(): pl.pallas_call(prep_kernel, out_shape=(jax.ShapeDtypeStruct((blocks, chan...  4.44 us

profile of v9, /device:TPU:1, one launch (start us, length us, event | category | flops | bytes accessed | tf_op | source)
XLA Modules:
  0.0 82.5 jit_solution(10486698314985320962)
XLA Ops:
  0.0 4.4 %prep.1 = (f32[1024,256]{1,0:T(8,128)S(1)}, f32[1024,256]{1,0:T(8,128)S(1)}, f32[1024,4]{1,0:T(8,128)S(1)}, f32[2,128,16384]{2,1,0:T(8,128)}) custom-call(s32[1,1024]{1,0:T(1,128)} %bitcast.5, bf16[2,1024,256]{2,1,0:T(8,128)(2,1)} %vis_hbm.1, bf16[2,1024]{1,0:T(2,128)(2,1)} %anchor_hbm.1, bf16[2,1024]{1,0:T(2,128)(2,1)} %drift_hbm.1), custom_call_target="tpu_custom_call" | custom-call | tf_op jit(solution)/shard_map/prep/pallas_call | solution.py:106
  4.4 73.1 %main.1 = (f32[2,16,64,128]{3,2,1,0:T(8,128)S(1)}, s32[16,128]{1,0:T(8,128)S(1)}) custom-call(s32[1,8]{1,0:T(1,128)} %bitcast.6, s32[1,8]{1,0:T(1,128)} %bitcast.7, s32[1,8]{1,0:T(1,128)} %bitcast.8, f32[1,8]{1,0:T(1,128)} %bitcast.9, bf16[128,128]{1,0:T(8,128)(2,1)} %constant.8.clone.left1_hbm, bf16[256,128]{1,0:T(8,128)(2,1)} %constant.9.clone.right1_hbm, ...), custom_call_target="tpu_custom_call" | custom-call | tf_op jit(solution)/shard_map/main/pallas_call | solution.py:564
  77.6 4.9 %deposit.1 = f32[2,128,16384]{2,1,0:T(8,128)} custom-call(s32[16,128]{1,0:T(8,128)S(1)} %get-tuple-element.14.table_ref, f32[2,16,64,128]{3,2,1,0:T(8,128)S(1)} %get-tuple-element.15.slot_ref, f32[2,128,16384]{2,1,0:T(8,128)} %get-tuple-element.16.grid_in), custom_call_target="tpu_custom_call", output_to_operand_aliasing={{}: (2, {})} | custom-call | tf_op jit(solution)/shard_map/deposit/pallas_call | solution.py:695

commit v10 on v8

--- a/solution.py
+++ b/solution.py
@@ -436,7 +436,8 @@
             prepare(i + 2, even)
             send[t, 2 * u + 1] = products(*odd).astype(BF16)
 
-        each(0, own // 2, two)
+        for u in range(own // 2):
+            two(u)
 
         @pl.when(t == 0)
         def _():

time: 86.9 us -> 76.6 us (0.88)
  the two profiles are of different devices: /device:TPU:1 before, /device:TPU:17 now
where the time goes in v10:
time: 76.6 us; the launch traced here: 76.5 us
  Pallas kernels  76.5 us (100%)
    pallas_call x1, Pallas kernels, main(): pl.pallas_call(functools.partial(main_kernel, nb, nf), out_shape=(jax.Sha...  63.3 us
    pallas_call x1, Pallas kernels, deposit(): pl.pallas_call(deposit_kernel, out_shape=jax.ShapeDtypeStruct((2, FR, GY)...  8.74 us
    pallas_call x1, Pallas kernels, prep(): pl.pallas_call(prep_kernel, out_shape=(jax.ShapeDtypeStruct((blocks, chan...  4.44 us

profile of v10, /device:TPU:17, one launch (start us, length us, event | category | flops | bytes accessed | tf_op | source)
XLA Modules:
  0.0 76.5 jit_solution(4078173446720291713)
XLA Ops:
  0.0 4.4 %prep.1 = (f32[1024,256]{1,0:T(8,128)S(1)}, f32[1024,256]{1,0:T(8,128)S(1)}, f32[1024,4]{1,0:T(8,128)S(1)}, f32[2,128,16384]{2,1,0:T(8,128)}) custom-call(s32[1,1024]{1,0:T(1,128)} %bitcast.5, bf16[2,1024,256]{2,1,0:T(8,128)(2,1)} %vis_hbm.1, bf16[2,1024]{1,0:T(2,128)(2,1)} %anchor_hbm.1, bf16[2,1024]{1,0:T(2,128)(2,1)} %drift_hbm.1), custom_call_target="tpu_custom_call" | custom-call | tf_op jit(solution)/shard_map/prep/pallas_call | solution.py:106
  4.4 63.3 %main.1 = (f32[2,16,64,128]{3,2,1,0:T(8,128)S(1)}, s32[16,128]{1,0:T(8,128)S(1)}) custom-call(s32[1,8]{1,0:T(1,128)} %bitcast.6, s32[1,8]{1,0:T(1,128)} %bitcast.7, s32[1,8]{1,0:T(1,128)} %bitcast.8, f32[1,8]{1,0:T(1,128)} %bitcast.9, bf16[128,128]{1,0:T(8,128)(2,1)} %constant.8.clone.left1_hbm, bf16[256,128]{1,0:T(8,128)(2,1)} %constant.9.clone.right1_hbm, ...), custom_call_target="tpu_custom_call" | custom-call | tf_op jit(solution)/shard_map/main/pallas_call | solution.py:546
  67.7 8.7 %deposit.1 = f32[2,128,16384]{2,1,0:T(8,128)} custom-call(s32[16,128]{1,0:T(8,128)S(1)} %get-tuple-element.14.table_ref, f32[2,16,64,128]{3,2,1,0:T(8,128)S(1)} %get-tuple-element.15.slot_ref, f32[2,128,16384]{2,1,0:T(8,128)} %get-tuple-element.16.grid_in), custom_call_target="tpu_custom_call", output_to_operand_aliasing={{}: (2, {})} | custom-call | tf_op jit(solution)/shard_map/deposit/pallas_call | solution.py:674
